TPU v7x, 32 devices: a whole 2x2x4 slice. The times are simulated.
32 devices in a mesh: seq: 8 (over z, core), chan: 4 (over y, x).
Axes of the slice: x: 2, y: 2, z: 4, core: 2. Of those that a mesh axis runs over, the one named last changes fastest.
Arguments:
- query_proj: bfloat16 [1024, 8192], P('seq', 'chan'), may hold values from -6 to 6
- key_proj: bfloat16 [1024, 8192], P('seq', 'chan'), may hold values from -6 to 6
- value_proj: bfloat16 [1024, 8192], P('seq', 'chan'), may hold values from -6 to 6
- short_filter: float32 [3, 512, 3], P(None, 'chan'), may hold values from -2.4 to 2.4
- long_filter: bfloat16 [512, 1024], P('chan'), may hold values from -4 to 4
- out_weight: bfloat16 [8192, 8192], P(None, 'chan'), may hold values from -0.09375 to 0.09375
- grad_out: bfloat16 [1024, 8192], P('seq', 'chan'), may hold values from -6 to 6
Outputs:
- mixer_out: bfloat16 [1024, 8192], P('seq', 'chan')
- grad_query: bfloat16 [1024, 8192], P('seq', 'chan')
- grad_key: bfloat16 [1024, 8192], P('seq', 'chan')
- grad_value: bfloat16 [1024, 8192], P('seq', 'chan')
All inputs are finite; a program needn't handle non-finite values.
Results may differ from a plain program's by a relative error of at most 0.0064.
Values may be sent and summed in bfloat16 or wider, within the bound.
A program may use at most 128 MiB of HBM per device.

v0:
```python
import jax
import jax.numpy as jnp
from jax import lax
from jax.sharding import PartitionSpec as P

GROUP = 16


def passed_along(array, axis, by):
    size = lax.axis_size(axis)
    pairs = [(i, i + by) for i in range(size) if 0 <= i + by < size]
    return lax.ppermute(array, axis, pairs)


def rim_rows(halo_part, offset):
    return passed_along(halo_part, "seq", offset)


def forward_taps(streams, per_chan):
    width = per_chan.shape[2] - 1
    tok_count = streams.shape[1]
    earlier = rim_rows(streams[:, tok_count - width :, :], 1)
    extended = jnp.concatenate([earlier, streams], axis=1)
    total = jnp.zeros(streams.shape, jnp.float32)
    for lag_index in range(width + 1):
        sliced = extended[:, width - lag_index : width - lag_index + tok_count, :]
        total = total + sliced.astype(jnp.float32) * per_chan[:, None, :, lag_index]
    return total


def backward_taps(grads, per_chan):
    width = per_chan.shape[2] - 1
    tok_count = grads.shape[1]
    later = rim_rows(grads[:, :width, :], -1)
    extended = jnp.concatenate([grads, later], axis=1)
    total = jnp.zeros(grads.shape, jnp.float32)
    for lag_index in range(width + 1):
        sliced = extended[:, lag_index : lag_index + tok_count, :]
        total = total + sliced.astype(jnp.float32) * per_chan[:, None, :, lag_index]
    return total


def to_channels(values):
    return lax.all_to_all(values, "seq", split_axis=1, concat_axis=0, tiled=True)


def to_tokens(values):
    return lax.all_to_all(values, "seq", split_axis=0, concat_axis=1, tiled=True)


def channel_filters(long_filter, chan_count):
    per_dev = chan_count // lax.axis_size("seq")
    group_width = min(per_dev, GROUP)
    group_count = per_dev // group_width
    first_group = lax.axis_index("seq") * per_dev // GROUP
    chosen = lax.dynamic_slice_in_dim(long_filter, first_group, group_count, 0)
    return (chosen, group_width)


def toeplitz_mix(values, chosen, group_width):
    length, chan_count = values.shape
    group_count = chosen.shape[0]
    block_len = min(256, length)
    nblocks = length // block_len
    blocked = values.T.reshape(group_count, group_width, nblocks, block_len)
    delayed = jnp.concatenate([jnp.zeros_like(blocked), blocked], axis=2)
    offsets = jnp.arange(block_len)[:, None] - jnp.arange(block_len)[None, :] + block_len
    padded = jnp.concatenate([jnp.zeros((group_count, block_len), chosen.dtype), chosen], axis=1)

    def add_lag(lag_block, totals):
        window = lax.dynamic_slice_in_dim(padded, lag_block * block_len, 2 * block_len, 1)
        kernel = window[:, offsets]
        source = lax.dynamic_slice_in_dim(delayed, nblocks - lag_block, nblocks, 2)
        return totals + jnp.einsum(
            "gab,gjnb->gjna", kernel, source, preferred_element_type=jnp.float32
        )

    start_sum = jnp.zeros((group_count, group_width, nblocks, block_len), jnp.float32)
    totals = lax.fori_loop(0, nblocks, add_lag, start_sum)
    return totals.reshape(chan_count, length).T


def project_out(gated, out_weight):
    return jnp.dot(
        lax.all_gather(gated, "chan", axis=1, tiled=True),
        out_weight,
        preferred_element_type=jnp.float32,
    ).astype(jnp.bfloat16)


def backward_partials(grad_out, out_weight):
    share = lax.psum_scatter(
        lax.dot_general(
            out_weight, grad_out, (((1,), (1,)), ((), ())), preferred_element_type=jnp.float32
        ),
        "chan",
        scatter_dimension=0,
        tiled=True,
    )
    return share.T


def local(query_proj, key_proj, value_proj, short_filter, long_filter, out_weight, grad_out):
    streams = jnp.stack([query_proj, key_proj, value_proj])
    per_chan = jnp.repeat(short_filter, GROUP, axis=1)
    filtered = forward_taps(streams, per_chan)
    query_f = filtered[0]
    key_f = filtered[1]
    value_f = filtered[2]
    products = (key_f * value_f).astype(jnp.bfloat16)
    chosen, group_width = channel_filters(long_filter, products.shape[1])
    mixed = to_tokens(toeplitz_mix(to_channels(products), chosen, group_width).astype(jnp.bfloat16))
    mixed_f = mixed.astype(jnp.float32)
    gated = (query_f * mixed_f).astype(jnp.bfloat16)
    mixer_out = project_out(gated, out_weight)
    grad_gated = backward_partials(grad_out, out_weight)
    grad_qf = (grad_gated * mixed_f).astype(jnp.bfloat16)
    grad_mixed = (grad_gated * query_f).astype(jnp.bfloat16)
    flipped = to_channels(grad_mixed)[::-1]
    grad_prod = to_tokens(toeplitz_mix(flipped, chosen, group_width)[::-1].astype(jnp.bfloat16))
    grad_pf = grad_prod.astype(jnp.float32)
    grad_kf = (grad_pf * value_f).astype(jnp.bfloat16)
    grad_vf = (grad_pf * key_f).astype(jnp.bfloat16)
    grads = backward_taps(jnp.stack([grad_qf, grad_kf, grad_vf]), per_chan).astype(jnp.bfloat16)
    return (mixer_out, grads[0], grads[1], grads[2])


def solution(mesh):
    return jax.shard_map(
        local,
        mesh=mesh,
        in_specs=(
            P("seq", "chan"),
            P("seq", "chan"),
            P("seq", "chan"),
            P(None, "chan", None),
            P("chan", None),
            P(None, "chan"),
            P("seq", "chan"),
        ),
        out_specs=(P("seq", "chan"), P("seq", "chan"), P("seq", "chan"), P("seq", "chan")),
        check_vma=False,
    )
```

profile of v0, /device:TPU:1, one launch (start us, length us, event | category | flops | bytes accessed | tf_op | source)
XLA Modules:
  0.0 2204.8 jit_solution(4532881256469032309)
XLA Ops:
  8.2 17.0 fusion.24
  25.3 1.0 copy-done.4
  28.5 4.6 collective-permute-start
  34.9 2.3 maximum_maximum_fusion
  37.3 5.3 multiply_add_fusion
  42.6 37.6 %reduce-scatter.2.cloned.1.call-done = f32[2048,128]{1,0:T(8,128)} async-done(((f32[8192,128]{1,0:T(8,128)}), f32[2048,128]{1,0:T(8,128)}) %reduce-scatter.2.cloned.1.call-update) | async-done | bytes 1048592 | tf_op jit(solution)/shard_map/reduce_scatter | solution.py:92
  80.2 1.6 fusion.21
  81.8 1.0 copy.56
  82.9 5.3 all-to-all-start.2
  89.2 13.4 all-to-all-done.2
  103.8 1.3 concatenate.19
  105.2 986.2 %while.33 = (s32[]{:T(128)}, f32[16,16,4,256]{3,1,2,0:T(8,128)}, bf16[16,16,8,256]{3,2,1,0:T(8,128)(2,1)}, bf16[16,1280]{0,1:T(8,128)(2,1)S(1)}, s32[]{:T(128)},...) while((s32[]{:T(128)}, f32[16,16,4,256]{3,1,2,0:T(8,128)}, ...), condition=%wide.region_4.5_spmd.clone, body=%wide.region_3.4_spmd.clone.sunk | while | flops 135135248 | bytes 15761619 | solution.py:79
  105.4 229.0 %gather_fusion.1 = bf16[65536,16]{1,0:T(8,128)(2,1)} fusion(bf16[16,512]{0,1:T(8,128)(2,1)S(1)} %constant_dynamic-slice_fusion.11, s32[65536]{0:T(1024)S(1)} %broadcast_clamp_fusion.5), kind=kCustom, calls=%fused_computation.1.clone.clone.1 | custom fusion | bytes 4456448 | tf_op jit(solution)/shard_map/while/body/eval_jaxpr/gather | solution.py:72
  334.4 13.1 copy.98
  347.5 1.5 constant_dynamic-slice_fusion.12
  349.0 1.7 fusion.44
  351.0 229.0 %gather_fusion.1 = bf16[65536,16]{1,0:T(8,128)(2,1)} fusion(bf16[16,512]{0,1:T(8,128)(2,1)S(1)} %constant_dynamic-slice_fusion.11, s32[65536]{0:T(1024)S(1)} %broadcast_clamp_fusion.5), kind=kCustom, calls=%fused_computation.1.clone.clone.1 | custom fusion | bytes 4456448 | tf_op jit(solution)/shard_map/while/body/eval_jaxpr/gather | solution.py:72
  580.0 13.1 copy.98
  593.1 1.5 constant_dynamic-slice_fusion.12
  594.7 3.0 fusion.44
  597.9 229.0 %gather_fusion.1 = bf16[65536,16]{1,0:T(8,128)(2,1)} fusion(bf16[16,512]{0,1:T(8,128)(2,1)S(1)} %constant_dynamic-slice_fusion.11, s32[65536]{0:T(1024)S(1)} %broadcast_clamp_fusion.5), kind=kCustom, calls=%fused_computation.1.clone.clone.1 | custom fusion | bytes 4456448 | tf_op jit(solution)/shard_map/while/body/eval_jaxpr/gather | solution.py:72
  826.8 13.1 copy.98
  839.9 1.5 constant_dynamic-slice_fusion.12
  841.5 3.0 fusion.44
  844.7 229.0 %gather_fusion.1 = bf16[65536,16]{1,0:T(8,128)(2,1)} fusion(bf16[16,512]{0,1:T(8,128)(2,1)S(1)} %constant_dynamic-slice_fusion.11, s32[65536]{0:T(1024)S(1)} %broadcast_clamp_fusion.5), kind=kCustom, calls=%fused_computation.1.clone.clone.1 | custom fusion | bytes 4456448 | tf_op jit(solution)/shard_map/while/body/eval_jaxpr/gather | solution.py:72
  1073.7 13.1 copy.98
  1086.8 1.5 constant_dynamic-slice_fusion.12
  1088.3 3.0 fusion.44
  1091.3 1.9 copy.59
  1093.4 1.7 rev.7
  1095.3 17.6 all_to_all.61
  1113.3 2.7 fusion.18
  1116.0 1.0 copy.49
  1117.0 4.4 all-to-all-start
  1121.4 14.5 all-to-all-done
  1136.5 1.3 concatenate.17
  1137.9 986.2 %while.32 = (s32[]{:T(128)}, f32[16,16,4,256]{3,1,2,0:T(8,128)}, bf16[16,16,8,256]{3,2,1,0:T(8,128)(2,1)}, bf16[16,1280]{0,1:T(8,128)(2,1)S(1)}, s32[]{:T(128)},...) while((s32[]{:T(128)}, f32[16,16,4,256]{3,1,2,0:T(8,128)}, ...), condition=%wide.region_1.2_spmd.clone, body=%wide.region_0.1_spmd.clone.sunk | while | flops 135135248 | bytes 15761619 | solution.py:79
  1138.1 229.0 %gather_fusion = bf16[65536,16]{1,0:T(8,128)(2,1)} fusion(bf16[16,512]{0,1:T(8,128)(2,1)S(1)} %constant_dynamic-slice_fusion.9, s32[65536]{0:T(1024)S(1)} %broadcast_clamp_fusion.4), kind=kCustom, calls=%fused_computation.clone.clone.1 | custom fusion | bytes 4456448 | tf_op jit(solution)/shard_map/while/body/eval_jaxpr/gather | solution.py:72
  1367.1 13.1 copy.95
  1380.2 1.5 constant_dynamic-slice_fusion.10
  1381.7 1.7 fusion.40
  1383.7 229.0 %gather_fusion = bf16[65536,16]{1,0:T(8,128)(2,1)} fusion(bf16[16,512]{0,1:T(8,128)(2,1)S(1)} %constant_dynamic-slice_fusion.9, s32[65536]{0:T(1024)S(1)} %broadcast_clamp_fusion.4), kind=kCustom, calls=%fused_computation.clone.clone.1 | custom fusion | bytes 4456448 | tf_op jit(solution)/shard_map/while/body/eval_jaxpr/gather | solution.py:72
  1612.7 13.1 copy.95
  1625.8 1.5 constant_dynamic-slice_fusion.10
  1627.4 3.0 fusion.40
  1630.6 229.0 %gather_fusion = bf16[65536,16]{1,0:T(8,128)(2,1)} fusion(bf16[16,512]{0,1:T(8,128)(2,1)S(1)} %constant_dynamic-slice_fusion.9, s32[65536]{0:T(1024)S(1)} %broadcast_clamp_fusion.4), kind=kCustom, calls=%fused_computation.clone.clone.1 | custom fusion | bytes 4456448 | tf_op jit(solution)/shard_map/while/body/eval_jaxpr/gather | solution.py:72
  1859.5 13.1 copy.95
  1872.7 1.5 constant_dynamic-slice_fusion.10
  1874.2 3.0 fusion.40
  1877.4 229.0 %gather_fusion = bf16[65536,16]{1,0:T(8,128)(2,1)} fusion(bf16[16,512]{0,1:T(8,128)(2,1)S(1)} %constant_dynamic-slice_fusion.9, s32[65536]{0:T(1024)S(1)} %broadcast_clamp_fusion.4), kind=kCustom, calls=%fused_computation.clone.clone.1 | custom fusion | bytes 4456448 | tf_op jit(solution)/shard_map/while/body/eval_jaxpr/gather | solution.py:72
  2106.4 13.1 copy.95
  2119.5 1.5 constant_dynamic-slice_fusion.10
  2121.0 3.0 fusion.40
  2124.0 1.3 convert_element_type.91
  2125.9 17.7 all_to_all.62
  2143.7 1.4 copy.55
  2145.1 2.5 fusion.20
  2148.5 3.2 collective-permute-start.1
  2151.7 2.0 collective-permute-done.1
  2155.3 3.9 add_convert_fusion
  2159.3 1.0 copy.64
  2160.3 1.0 copy.65
  2162.3 19.0 all-gather.2.cloned.1.call-done
  2181.4 16.5 convolution_convert_fusion
  (92 shorter events, 14.5 us)
Async XLA Ops:
  7.2 1.1 copy-start
  7.2 73.0 %reduce-scatter.2.cloned.1.call-start = ((), (), s32[]{:S(2)}) async-start(), calls=%async_computation.6 | async-start | bytes 5242880 | tf_op jit(solution)/shard_map/reduce_scatter | solution.py:92
  25.2 1.0 copy-start.4
  25.2 1.3 copy-start.5
  25.2 1.6 copy-start.6
  27.3 5.8 copy-start.9
  28.5 5.5 collective-permute-start
  33.8 3.5 copy-start.7
  82.9 19.8 all-to-all-start.2
  1117.0 18.9 all-to-all-start
  1121.4 1059.9 %all-gather.2.cloned.1.call-start = ((), (), s32[]{:S(2)}) async-start(), calls=%async_computation.5 | async-start | bytes 2621440 | tf_op jit(solution)/shard_map/all_gather | solution.py:85
  2125.7 19.4 copy-start.3
  2143.7 3.9 copy-start.2
  2148.5 5.1 collective-permute-start.1
  2154.6 0.8 copy-start.8
  2181.4 16.6 copy-start.1
Sparse Core Ops, SparseCore 0:
  25.4 54.7 reduce-scatter.1
  2147.8 33.5 all-gather.1
where the time goes:
time: 2210 us; the launch traced here: 2200 us
  local copies, waits for them, and re-layouts  1970 us (89%)
  waiting for transfers between devices  86.8 us (4%)
  matrix products  54.8 us (2%)
  blocking collectives  35.3 us (2%)
    gather x16, local copies, waits for them, and re-layouts, add_lag(): kernel = window[:, offsets]  1940 us
  transfers between devices with their start and end apart: 6, of which 6 were waited for; matrix products, arithmetic and copies ran while one was open for 1% of the time, Pallas kernels for 0%

commit v1 on v0

v1 whole, which is shorter than its diff:
```python
import functools

import jax
import jax.numpy as jnp
from jax import lax
from jax.experimental import pallas as pl
from jax.experimental.pallas import tpu as pltpu
from jax.sharding import PartitionSpec as P

GROUP = 16
F32 = jnp.float32
BF16 = jnp.bfloat16


def passed_along(array, by):
    size = lax.axis_size("seq")
    pairs = [(i, i + by) for i in range(size) if 0 <= i + by < size]
    return lax.ppermute(array, "seq", pairs)


def causal(x, before, taps):
    row = lax.broadcasted_iota(jnp.int32, x.shape, 0)
    one = jnp.where(row == 0, before[1:2], pltpu.roll(x, 1, 0))
    two = jnp.where(row == 0, before[0:1], jnp.where(row == 1, before[1:2], pltpu.roll(x, 2, 0)))
    return x * taps[0:1] + one * taps[1:2] + two * taps[2:3]


def anticausal(g, after, taps):
    count = g.shape[0]
    row = lax.broadcasted_iota(jnp.int32, g.shape, 0)
    one = jnp.where(row == count - 1, after[0:1], pltpu.roll(g, count - 1, 0))
    two = jnp.where(
        row == count - 1,
        after[1:2],
        jnp.where(row == count - 2, after[0:1], pltpu.roll(g, count - 2, 0)),
    )
    return g * taps[0:1] + one * taps[1:2] + two * taps[2:3]


def products_kernel(k_ref, v_ref, before_ref, taps_ref, out_ref):
    before = before_ref[...].astype(F32)
    kf = causal(k_ref[...].astype(F32), before[2:4], taps_ref[3:6])
    vf = causal(v_ref[...].astype(F32), before[4:6], taps_ref[6:9])
    out_ref[...] = (kf * vf).T.astype(BF16)


def toeplitz_kernel(h_ref, hr_ref, fwd_ref, bwd_ref):
    groups, length = h_ref.shape
    block = fwd_ref.shape[2]
    for g in range(groups):
        pad = jnp.zeros((block, block), F32)
        rows = jnp.broadcast_to(h_ref[g : g + 1, :].astype(F32), (block, length))
        lined = pltpu.roll(
            jnp.concatenate([pad, rows], axis=1), 0, 1, stride=1, stride_axis=0
        ).astype(BF16)
        for k in range(length // block):
            fwd_ref[g, k * block : (k + 1) * block, :] = lined[:, (k + 1) * block : (k + 2) * block]
        rows = jnp.broadcast_to(hr_ref[g : g + 1, :].astype(F32), (block, length))
        lined = pltpu.roll(
            jnp.concatenate([rows, pad], axis=1), 1, 1, stride=1, stride_axis=0
        ).astype(BF16)
        for k in range(length // block):
            at = length - k * block
            bwd_ref[g, k * block : (k + 1) * block, :] = lined[:, at : at + block]


def mix_kernel(forward, x_ref, filt_ref, out_ref):
    blocks, groups, width, block = x_ref.shape
    rows = blocks * width
    for g in range(groups):
        x = x_ref[:, g]
        if width % 16:
            x = x.astype(F32)
        x = x.reshape(rows, block).astype(BF16)
        parts = [x]
        for k in range(1, blocks):
            pad = jnp.zeros((k * width, block), F32 if width % 16 else BF16)
            src = x.astype(pad.dtype)
            if forward:
                moved = jnp.concatenate([pad, src[: rows - k * width]], axis=0)
            else:
                moved = jnp.concatenate([src[k * width :], pad], axis=0)
            parts.append(moved.astype(BF16))
        total = jnp.dot(
            jnp.concatenate(parts, axis=1), filt_ref[g], preferred_element_type=F32
        )
        out_ref[:, g] = total.reshape(blocks, width, block).astype(BF16)


def gate_kernel(q_ref, before_ref, taps_ref, mixed_ref, out_ref):
    qf = causal(q_ref[...].astype(F32), before_ref[...].astype(F32)[0:2], taps_ref[0:3])
    out_ref[...] = (qf * mixed_ref[...].astype(F32).T).astype(BF16)


def grad_mixed_kernel(q_ref, before_ref, taps_ref, parts_ref, out_ref):
    qf = causal(q_ref[...].astype(F32), before_ref[...].astype(F32)[0:2], taps_ref[0:3])
    total = jnp.sum(parts_ref[...].astype(F32), axis=0)
    out_ref[...] = (total * qf.T).astype(BF16)


def grad_query_kernel(mixed_ref, parts_ref, out_ref):
    total = jnp.sum(parts_ref[...].astype(F32), axis=0)
    out_ref[...] = (total * mixed_ref[...].astype(F32)).T.astype(BF16)


def last_kernel(
    k_ref, v_ref, before_ref, after_ref, taps_ref, gqf_ref, gqf_next_ref, gp_ref, gp_next_ref,
    gq_ref, gk_ref, gv_ref,
):
    count = k_ref.shape[0]
    before = before_ref[...].astype(F32)
    after = after_ref[...].astype(F32)
    gqf_next = gqf_next_ref[...].astype(F32)
    gp_next = gp_next_ref[...].astype(F32)

    def rounded(x):
        return x.astype(BF16).astype(F32)

    def filtered(ref, at):
        x = ref[...].astype(F32)
        taps = taps_ref[3 * at : 3 * at + 3]
        new = after[2 * at - 2 : 2 * at]
        f = causal(x, before[2 * at : 2 * at + 2], taps)
        last, ahead = x[count - 1 : count], x[count - 2 : count - 1]
        first = new[0:1] * taps[0:1] + last * taps[1:2] + ahead * taps[2:3]
        second = new[1:2] * taps[0:1] + new[0:1] * taps[1:2] + last * taps[2:3]
        return f, jnp.concatenate([first, second], axis=0)

    kf, kf_next = filtered(k_ref, 1)
    vf, vf_next = filtered(v_ref, 2)
    gp = gp_ref[...].astype(F32).T
    gq_ref[...] = anticausal(gqf_ref[...].astype(F32), gqf_next, taps_ref[0:3]).astype(BF16)
    gk_ref[...] = anticausal(
        rounded(gp * vf), rounded(gp_next * vf_next), taps_ref[3:6]
    ).astype(BF16)
    gv_ref[...] = anticausal(
        rounded(gp * kf), rounded(gp_next * kf_next), taps_ref[6:9]
    ).astype(BF16)


def params(mib=48):
    return pltpu.CompilerParams(vmem_limit_bytes=mib * 1024 * 1024)


def cost(flops, nbytes):
    return pl.CostEstimate(flops=flops, bytes_accessed=nbytes, transcendentals=0)


def local(query_proj, key_proj, value_proj, short_filter, long_filter, out_weight, grad_out):
    count, width = query_proj.shape
    seq = lax.axis_size("seq")
    chan = lax.axis_size("chan")
    per = width // seq
    gw = min(per, GROUP)
    groups = per // gw
    length = long_filter.shape[1]
    tile = min(512, width)
    steps = width // tile

    taps = jnp.repeat(short_filter.transpose(0, 2, 1).reshape(9, -1), GROUP, axis=1)
    before = passed_along(
        jnp.concatenate([a[count - 2 :] for a in (query_proj, key_proj, value_proj)], axis=0), 1
    )
    after = passed_along(jnp.concatenate([a[:2] for a in (key_proj, value_proj)], axis=0), -1)
    first = lax.axis_index("seq") * per // GROUP
    chosen = lax.dynamic_slice_in_dim(long_filter, first, groups, 0)

    def tall(rows):
        return pl.BlockSpec((rows, tile), lambda i: (0, i))

    wide = pl.BlockSpec((tile, count), lambda i: (i, 0))
    stacked = pl.BlockSpec((chan, tile, count), lambda i: (0, i, 0))
    flat = jax.ShapeDtypeStruct((count, width), BF16)
    turned = jax.ShapeDtypeStruct((width, count), BF16)
    size = 2 * count * width

    parts = lax.dot_general(
        out_weight, grad_out, (((1,), (1,)), ((), ())), preferred_element_type=F32
    ).astype(BF16)
    parts = lax.all_to_all(parts.reshape(chan, width, count), "chan", 0, 0)

    products = pl.pallas_call(
        products_kernel,
        grid=(steps,),
        in_specs=[tall(count), tall(count), tall(6), tall(9)],
        out_specs=wide,
        out_shape=turned,
        compiler_params=params(),
        cost_estimate=cost(12 * count * width, 3 * size),
        name="products",
    )(key_proj, value_proj, before, taps)

    some = min(groups, 4)
    fwd_filt, bwd_filt = pl.pallas_call(
        toeplitz_kernel,
        grid=(max(1, groups // 8),),
        in_specs=[pl.BlockSpec((min(8, groups), length), lambda i: (i, 0))] * 2,
        out_specs=[pl.BlockSpec((min(8, groups), length, count), lambda i: (i, 0, 0))] * 2,
        out_shape=[jax.ShapeDtypeStruct((groups, length, count), BF16)] * 2,
        compiler_params=params(),
        cost_estimate=cost(20 * groups * length * count, 4 * groups * length * count),
        name="toeplitz",
    )(chosen, chosen[:, ::-1])

    def mix(values, filt, forward):
        values = lax.all_to_all(values.reshape(seq, per, count), "seq", 0, 0)
        spec = pl.BlockSpec((seq, some, gw, count), lambda i: (0, i, 0, 0))
        out = pl.pallas_call(
            functools.partial(mix_kernel, forward),
            grid=(groups // some,),
            in_specs=[spec, pl.BlockSpec((some, length, count), lambda i: (i, 0, 0))],
            out_specs=spec,
            out_shape=jax.ShapeDtypeStruct((seq, groups, gw, count), BF16),
            compiler_params=params(),
            cost_estimate=cost(
                2 * groups * seq * gw * length * count, 2 * size + 2 * groups * length * count
            ),
            name="mix",
        )(values.reshape(seq, groups, gw, count), filt)
        return lax.all_to_all(out.reshape(seq, per, count), "seq", 0, 0).reshape(width, count)

    mixed = mix(products, fwd_filt, True)

    grad_mixed = pl.pallas_call(
        grad_mixed_kernel,
        grid=(steps,),
        in_specs=[tall(count), tall(6), tall(9), stacked],
        out_specs=wide,
        out_shape=turned,
        compiler_params=params(),
        cost_estimate=cost(12 * count * width, (2 + chan) * size),
        name="grad_mixed",
    )(query_proj, before, taps, parts)
    grad_prod = mix(grad_mixed, bwd_filt, False)

    gated = pl.pallas_call(
        gate_kernel,
        grid=(steps,),
        in_specs=[tall(count), tall(6), tall(9), wide],
        out_specs=tall(count),
        out_shape=flat,
        compiler_params=params(),
        cost_estimate=cost(8 * count * width, 3 * size),
        name="gate",
    )(query_proj, before, taps, mixed)
    mixer_out = jnp.dot(
        lax.all_gather(gated, "chan", axis=1, tiled=True),
        out_weight,
        preferred_element_type=F32,
    ).astype(BF16)

    grad_qf = pl.pallas_call(
        grad_query_kernel,
        grid=(steps,),
        in_specs=[wide, stacked],
        out_specs=tall(count),
        out_shape=flat,
        compiler_params=params(),
        cost_estimate=cost(8 * count * width, (2 + chan) * size),
        name="grad_query",
    )(mixed, parts)
    grad_qf_next = passed_along(grad_qf[:2], -1)
    grad_prod_next = passed_along(grad_prod[:, :2].T, -1)

    grads = pl.pallas_call(
        last_kernel,
        grid=(steps,),
        in_specs=[
            tall(count), tall(count), tall(6), tall(4), tall(9), tall(count), tall(2), wide, tall(2),
        ],
        out_specs=[tall(count)] * 3,
        out_shape=[flat] * 3,
        compiler_params=params(),
        cost_estimate=cost(40 * count * width, 7 * size),
        name="last",
    )(
        key_proj, value_proj, before, after, taps, grad_qf, grad_qf_next, grad_prod, grad_prod_next
    )
    return (mixer_out, *grads)


def solution(mesh):
    return jax.shard_map(
        local,
        mesh=mesh,
        in_specs=(
            P("seq", "chan"),
            P("seq", "chan"),
            P("seq", "chan"),
            P(None, "chan", None),
            P("chan", None),
            P(None, "chan"),
            P("seq", "chan"),
        ),
        out_specs=(P("seq", "chan"), P("seq", "chan"), P("seq", "chan"), P("seq", "chan")),
        check_vma=False,
    )
```

time: 2210 us -> 183 us (0.08)
  local copies, waits for them, and re-layouts: 1970 us -> 21.7 us
  waiting for transfers between devices: 86.8 us -> 45.6 us
    gather x16 -> x0, local copies, waits for them, and re-layouts: 1940 us -> none  [add_lag(): kernel = window[:, offsets]]
    reduce_scatter x1 -> x0, waiting for transfers between devices: 37.6 us -> none  [backward_partials(): lax.psum_scatter(lax.dot_general(out_weight, grad_out, (((1,), (1,)), (()...]
    dot_general x10 -> x2, matrix products: 54.8 us -> 33.1 us  [the longest x1 16.7 us: local(): lax.dot_general(out_weight, grad_out, (((1,), (1,)), ((), ())), preferred...]
  transfers between devices with their start and end apart: 6 -> 9, of which waited for: 6 -> 4; matrix products, arithmetic and copies ran while one was open for 1% -> 13% of each run, Pallas kernels for 0% -> 7%
where the time goes in v1:
time: 183 us; the launch traced here: 182 us
  waiting for transfers between devices  45.6 us (25%)
  matrix products  33.1 us (18%)
  starting transfers between devices  30.2 us (17%)
  local copies, waits for them, and re-layouts  21.7 us (12%)
  blocking collectives  20.1 us (11%)
  Pallas kernels  17.1 us (9%)
  between operations  14.2 us (8%)
    all_to_all x1, waiting for transfers between devices, local(): parts = lax.all_to_all(parts.reshape(chan, width, count), 'chan', 0, 0)  27.7 us
    all_to_all x1, blocking collectives, mix(): values = lax.all_to_all(values.reshape(seq, per, count), 'seq', 0, 0)  20.1 us
    dot_general x1, matrix products, local(): lax.dot_general(out_weight, grad_out, (((1,), (1,)), ((), ())), preferred...  16.7 us
    dot_general x1, matrix products, local(): jnp.dot(lax.all_gather(gated, 'chan', axis=1, tiled=True), out_weight, pr...  16.5 us
    unnamed x28, local copies, waits for them, and re-layouts  13.9 us
    ppermute x4, starting transfers between devices, passed_along(): return lax.ppermute(array, 'seq', pairs)  11.5 us
    all_to_all x2, starting transfers between devices, mix(): lax.all_to_all(out.reshape(seq, per, count), 'seq', 0, 0)  9.33 us
    all_to_all x2, waiting for transfers between devices, mix(): lax.all_to_all(out.reshape(seq, per, count), 'seq', 0, 0)  8.94 us
  transfers between devices with their start and end apart: 9, of which 4 were waited for; matrix products, arithmetic and copies ran while one was open for 13% of the time, Pallas kernels for 7%

profile of v1, /device:TPU:1, one launch (start us, length us, event | category | flops | bytes accessed | tf_op | source)
XLA Modules:
  0.0 182.1 jit_solution(15645998423468096987)
XLA Ops:
  7.2 0.0 copy-start
  7.2 0.8 slice.21
  8.0 0.8 fusion
  8.9 4.6 %collective-permute-start = (bf16[6,2048]{1,0:T(8,128)(2,1)S(1)}, bf16[6,2048]{1,0:T(8,128)(2,1)S(1)}, u32[]{:S(2)}, u32[]{:S(2)}) collective-permute-start(bf16[6,2048]{1,0:T(8,128)(2,1)S(1)} %pad_maximum_fusion), channel_id=1, source_target_pairs={{0,4},{4,8},{8,12},{12,16},{16,20},{20,24},{24,28},{1,5},{5,9},{9,... | collective-permute-start | bytes 73736 | tf_op jit(solution)/shard_map/ppermute | solution.py:18
  13.5 0.7 reshape.41
  14.2 0.2 broadcast_in_dim.3
  14.4 0.3 reshape.42.taps_ref
  14.8 0.0 collective-permute-done.before_ref
  14.8 0.0 copy-start.4
  14.8 1.0 copy-done.4
  15.8 0.0 copy-start.6
  15.8 1.0 copy-done.6
  16.8 2.3 %products.1 = bf16[2048,128]{1,0:T(8,128)(2,1)} custom-call(bf16[128,2048]{1,0:T(8,128)(2,1)S(1)} %copy-done.4, bf16[128,2048]{1,0:T(8,128)(2,1)S(1)} %copy-done.6, bf16[6,2048]{1,0:T(8,128)(2,1)S(1)} %collective-permute-done.before_ref, f32[9,2048]{1,0:T(8,128)S(1)} %reshape.42.taps_ref), custom_call_target="tpu_custom_call" | custom-call | flops 3145728 | bytes 1572864 | tf_op jit(solution)/shard_map/products/pallas_call | solution.py:182
  19.1 5.7 %all-to-all-start = ((bf16[8,256,128]{2,1,0:T(8,128)(2,1)}), bf16[8,256,128]{2,1,0:T(8,128)(2,1)S(1)}, u32[]{:S(2)}, u32[]{:S(2)}) async-start(bf16[8,256,128]{2,1,0:T(8,128)(2,1)} %bitcast.1), calls=%async_computation | async-start | bytes 1048576 | tf_op jit(solution)/shard_map/all_to_all | solution.py:206
  24.9 0.8 constant_dynamic-slice_fusion.h_ref
  25.7 0.7 rev.3.hr_ref
  26.3 3.8 %toeplitz.1 = (bf16[16,1024,128]{2,1,0:T(8,128)(2,1)S(1)}, bf16[16,1024,128]{2,1,0:T(8,128)(2,1)}) custom-call(bf16[16,1024]{1,0:T(8,128)(2,1)S(1)} %constant_dynamic-slice_fusion.h_ref, bf16[16,1024]{1,0:T(8,128)(2,1)S(1)} %rev.3.hr_ref), custom_call_target="tpu_custom_call" | custom-call | flops 41943040 | bytes 8388608 | tf_op jit(solution)/shard_map/toeplitz/pallas_call | solution.py:194
  30.1 0.0 copy-start.2
  30.1 2.0 %copy-done.2 = bf16[16,1024,128]{2,1,0:T(8,128)(2,1)} copy-done((bf16[16,1024,128]{2,1,0:T(8,128)(2,1)}, bf16[16,1024,128]{2,1,0:T(8,128)(2,1)S(1)}, u32[]{:S(2)}) %copy-start.2) | copy-done | bytes 4194328
  32.2 7.2 %all-to-all-done = bf16[8,256,128]{2,1,0:T(8,128)(2,1)S(1)} async-done(((bf16[8,256,128]{2,1,0:T(8,128)(2,1)}), bf16[8,256,128]{2,1,0:T(8,128)(2,1)S(1)}, u32[]{:S(2)}, u32[]{:S(2)}) %all-to-all-start) | async-done | bytes 524320 | tf_op jit(solution)/shard_map/all_to_all | solution.py:206
  39.4 0.0 copy-start.3
  39.4 2.2 %copy-done.3 = bf16[16,1024,128]{2,1,0:T(8,128)(2,1)S(1)} copy-done((bf16[16,1024,128]{2,1,0:T(8,128)(2,1)S(1)}, bf16[16,1024,128]{2,1,0:T(8,128)(2,1)}, u32[]{:S(2)}) %copy-start.3) | copy-done | bytes 4194328
  41.5 2.7 %mix.2 = bf16[8,16,16,128]{3,2,1,0:T(8,128)(2,1)} custom-call(bf16[8,16,16,128]{3,2,1,0:T(8,128)(2,1)S(1)} %bitcast.19, bf16[16,1024,128]{2,1,0:T(8,128)(2,1)S(1)} %copy-done.3), custom_call_target="tpu_custom_call" | custom-call | flops 536870912 | bytes 5242880 | tf_op jit(solution)/shard_map/mix/pallas_call | solution.py:208
  44.2 4.3 %all-to-all-start.1 = ((bf16[8,256,128]{2,1,0:T(8,128)(2,1)}), bf16[8,256,128]{2,1,0:T(8,128)(2,1)S(1)}, u32[]{:S(2)}, u32[]{:S(2)}) async-start(bf16[8,256,128]{2,1,0:T(8,128)(2,1)} %bitcast.3), calls=%async_computation.1 | async-start | bytes 1048576 | tf_op jit(solution)/shard_map/all_to_all | solution.py:220
  48.5 0.0 copy-done
  48.5 16.7 %convolution_convert_fusion = bf16[8192,128]{1,0:T(8,128)(2,1)} fusion(bf16[8192,2048]{1,0:T(8,128)(2,1)} %param.12, bf16[128,2048]{1,0:T(8,128)(2,1)S(1)} %copy-done), kind=kOutput, calls=%fused_computation | convolution fusion | flops 4296015872 | bytes 36175872 | tf_op jit(solution)/shard_map/dot_general | solution.py:177
  65.1 0.0 all-to-all-done.1
  65.1 3.6 %all-to-all-start.2 = ((bf16[4,2048,128]{2,1,0:T(8,128)(2,1)}), bf16[4,2048,128]{2,1,0:T(8,128)(2,1)S(1)}, u32[]{:S(2)}, u32[]{:S(2)}) async-start(bf16[4,2048,128]{2,1,0:T(8,128)(2,1)} %bitcast.25), calls=%async_computation.2 | async-start | bytes 4194304 | tf_op jit(solution)/shard_map/all_to_all | solution.py:180
  68.8 0.0 all-gather.2.cloned.1.call-start
  68.8 0.0 copy-start.8
  68.8 1.0 copy-done.8
  69.9 0.7 gate.1
  70.5 0.0 copy-start.13
  70.5 0.8 copy-done.13
  71.3 0.0 all-gather.2.cloned.1.call-update
  71.4 27.7 %all-to-all-done.2.parts_ref = bf16[4,2048,128]{2,1,0:T(8,128)(2,1)S(1)} async-done(((bf16[4,2048,128]{2,1,0:T(8,128)(2,1)}), bf16[4,2048,128]{2,1,0:T(8,128)(2,1)S(1)}, u32[]{:S(2)}, u32[]{:S(2)}) %all-to-all-start.2) | async-done | bytes 2097184 | tf_op jit(solution)/shard_map/all_to_all | solution.py:180
  99.1 0.0 copy-start.9
  99.1 1.0 copy-done.9
  100.1 0.0 copy-start.1
  100.1 0.9 grad_mixed.1
  101.0 20.1 %all_to_all.25 = bf16[8,256,128]{2,1,0:T(8,128)(2,1)S(1)} all-to-all(bf16[8,256,128]{2,1,0:T(8,128)(2,1)S(1)} %bitcast.22), channel_id=1, replica_groups=mesh['seq'=8,'chan'=4] {'seq'}, dimensions={0} | all-to-all | bytes 1048576 | tf_op jit(solution)/shard_map/all_to_all | solution.py:206
  121.2 0.0 copy-done.1
  121.2 1.8 %mix.3 = bf16[8,16,16,128]{3,2,1,0:T(8,128)(2,1)S(1)} custom-call(bf16[8,16,16,128]{3,2,1,0:T(8,128)(2,1)S(1)} %bitcast.20, bf16[16,1024,128]{2,1,0:T(8,128)(2,1)S(1)} %copy-done.1), custom_call_target="tpu_custom_call" | custom-call | flops 536870912 | bytes 5242880 | tf_op jit(solution)/shard_map/mix/pallas_call | solution.py:208
  123.0 0.0 copy-start.12
  123.0 0.8 copy-done.12
  123.8 2.0 %copy.15 = bf16[8,256,128]{1,2,0:T(8,128)(2,1)} copy(bf16[8,256,128]{2,1,0:T(8,128)(2,1)} %bitcast.21) | data formatting | bytes 1048576 | tf_op jit(solution)/shard_map/reshape | solution.py:220
  125.8 5.1 %all-to-all-start.4 = ((bf16[8,256,128]{1,2,0:T(8,128)(2,1)}), bf16[8,256,128]{1,2,0:T(8,128)(2,1)}, u32[]{:S(2)}, u32[]{:S(2)}) async-start(bf16[8,256,128]{1,2,0:T(8,128)(2,1)} %copy.15), calls=%async_computation.4 | async-start | bytes 1048576 | tf_op jit(solution)/shard_map/all_to_all | solution.py:220
  130.9 2.0 %collective-permute-start.1 = (bf16[4,2048]{1,0:T(4,128)(2,1)S(1)}, bf16[4,2048]{1,0:T(4,128)(2,1)S(1)}, u32[]{:S(2)}, u32[]{:S(2)}) collective-permute-start(bf16[4,2048]{1,0:T(4,128)(2,1)S(1)} %pad_maximum_fusion.1), channel_id=1, source_target_pairs={{4,0},{8,4},{12,8},{16,12},{20,16},{24,20},{28,24},{5,1},{9,5},{13... | collective-permute-start | bytes 49160 | tf_op jit(solution)/shard_map/ppermute | solution.py:18
  133.0 0.9 grad_query.1.gqf_ref
  133.9 0.0 copy-start.10
  133.9 0.8 copy-done.10
  134.7 1.9 %collective-permute-start.2 = (bf16[2,2048]{1,0:T(2,128)(2,1)S(1)}, bf16[2,2048]{1,0:T(2,128)(2,1)S(1)}, u32[]{:S(2)}, u32[]{:S(2)}) collective-permute-start(bf16[2,2048]{1,0:T(2,128)(2,1)S(1)} %slice.28), channel_id=1, source_target_pairs={{4,0},{8,4},{12,8},{16,12},{20,16},{24,20},{28,24},{5,1},{9,5},{13... | collective-permute-start | bytes 24584 | tf_op jit(solution)/shard_map/ppermute | solution.py:18
  136.6 8.9 %all-to-all-done.4 = bf16[8,256,128]{1,2,0:T(8,128)(2,1)} async-done(((bf16[8,256,128]{1,2,0:T(8,128)(2,1)}), bf16[8,256,128]{1,2,0:T(8,128)(2,1)}, u32[]{:S(2)}, u32[]{:S(2)}) %all-to-all-start.4) | async-done | bytes 524320 | tf_op jit(solution)/shard_map/all_to_all | solution.py:220
  145.5 1.1 copy.18
  146.6 3.0 %collective-permute-start.3 = (bf16[2,2048]{1,0:T(2,128)(2,1)S(1)}, bf16[2,2048]{1,0:T(2,128)(2,1)S(1)}, u32[]{:S(2)}, u32[]{:S(2)}) collective-permute-start(bf16[2,2048]{1,0:T(2,128)(2,1)S(1)} %slice_bitcast_fusion), channel_id=1, source_target_pairs={{4,0},{8,4},{12,8},{16,12},{20,16},{24,20},{28,24},{5,1},{9,5},{13... | collective-permute-start | bytes 24584 | tf_op jit(solution)/shard_map/ppermute | solution.py:18
  149.6 0.3 copy.17.gp_ref
  149.9 0.0 collective-permute-done.1.after_ref
  149.9 0.0 collective-permute-done.2.gqf_next_ref
  149.9 1.7 collective-permute-done.3.gp_next_ref
  151.6 1.0 copy-done.5
  152.7 1.0 copy-done.7
  153.7 1.0 copy-done.11
  154.7 4.1 %last.1 = (bf16[128,2048]{1,0:T(8,128)(2,1)}, bf16[128,2048]{1,0:T(8,128)(2,1)}, bf16[128,2048]{1,0:T(8,128)(2,1)}) custom-call(bf16[128,2048]{1,0:T(8,128)(2,1)S(1)} %copy-done.5, bf16[128,2048]{1,0:T(8,128)(2,1)S(1)} %copy-done.7, bf16[6,2048]{1,0:T(8,128)(2,1)S(1)} %collective-permute-done.before_ref, ...), custom_call_target="tpu_custom_call" | custom-call | flops 10485760 | bytes 3670016 | tf_op jit(solution)/shard_map/last/pallas_call | solution.py:265
  158.8 16.5 %convolution_convert_fusion.1 = bf16[128,2048]{1,0:T(8,128)(2,1)} fusion(bf16[128,8192]{1,0:T(8,128)(2,1)} %all-gather.2.cloned.1.call-done, bf16[8192,2048]{1,0:T(8,128)(2,1)} %param.12), kind=kOutput, calls=%fused_computation.1 | convolution fusion | flops 4295229440 | bytes 36175872 | tf_op jit(solution)/shard_map/dot_general | solution.py:246
  (8 shorter events, 0.1 us)
Async XLA Ops:
  7.2 41.3 %copy-start = (bf16[128,2048]{1,0:T(8,128)(2,1)S(1)}, bf16[128,2048]{1,0:T(8,128)(2,1)}, u32[]{:S(2)}) copy-start(bf16[128,2048]{1,0:T(8,128)(2,1)} %param.13) | copy-start | bytes 1572868
  8.9 5.9 %collective-permute-start = (bf16[6,2048]{1,0:T(8,128)(2,1)S(1)}, bf16[6,2048]{1,0:T(8,128)(2,1)S(1)}, u32[]{:S(2)}, u32[]{:S(2)}) collective-permute-start(bf16[6,2048]{1,0:T(8,128)(2,1)S(1)} %pad_maximum_fusion), channel_id=1, source_target_pairs={{0,4},{4,8},{8,12},{12,16},{16,20},{20,24},{24,28},{1,5},{5,9},{9,... | collective-permute-start | bytes 73736 | tf_op jit(solution)/shard_map/ppermute | solution.py:18
  14.8 1.0 copy-start.4
  15.8 1.0 copy-start.6
  19.1 20.2 %all-to-all-start = ((bf16[8,256,128]{2,1,0:T(8,128)(2,1)}), bf16[8,256,128]{2,1,0:T(8,128)(2,1)S(1)}, u32[]{:S(2)}, u32[]{:S(2)}) async-start(bf16[8,256,128]{2,1,0:T(8,128)(2,1)} %bitcast.1), calls=%async_computation | async-start | bytes 1048576 | tf_op jit(solution)/shard_map/all_to_all | solution.py:206
  30.1 2.0 %copy-start.2 = (bf16[16,1024,128]{2,1,0:T(8,128)(2,1)}, bf16[16,1024,128]{2,1,0:T(8,128)(2,1)S(1)}, u32[]{:S(2)}) copy-start(bf16[16,1024,128]{2,1,0:T(8,128)(2,1)S(1)} %get-tuple-element.9.filt_ref) | copy-start | bytes 12582916
  39.4 2.2 %copy-start.3 = (bf16[16,1024,128]{2,1,0:T(8,128)(2,1)S(1)}, bf16[16,1024,128]{2,1,0:T(8,128)(2,1)}, u32[]{:S(2)}) copy-start(bf16[16,1024,128]{2,1,0:T(8,128)(2,1)} %copy-done.2) | copy-start | bytes 12582916
  44.2 20.9 %all-to-all-start.1 = ((bf16[8,256,128]{2,1,0:T(8,128)(2,1)}), bf16[8,256,128]{2,1,0:T(8,128)(2,1)S(1)}, u32[]{:S(2)}, u32[]{:S(2)}) async-start(bf16[8,256,128]{2,1,0:T(8,128)(2,1)} %bitcast.3), calls=%async_computation.1 | async-start | bytes 1048576 | tf_op jit(solution)/shard_map/all_to_all | solution.py:220
  65.1 33.9 %all-to-all-start.2 = ((bf16[4,2048,128]{2,1,0:T(8,128)(2,1)}), bf16[4,2048,128]{2,1,0:T(8,128)(2,1)S(1)}, u32[]{:S(2)}, u32[]{:S(2)}) async-start(bf16[4,2048,128]{2,1,0:T(8,128)(2,1)} %bitcast.25), calls=%async_computation.2 | async-start | bytes 4194304 | tf_op jit(solution)/shard_map/all_to_all | solution.py:180
  68.8 90.0 %all-gather.2.cloned.1.call-start = ((), (), s32[]{:S(2)}) async-start(), calls=%async_computation.5 | async-start | bytes 2621440 | tf_op jit(solution)/shard_map/all_gather | solution.py:247
  68.8 1.0 copy-start.8
  70.5 0.8 copy-start.13
  99.1 1.0 copy-start.9
  100.1 21.1 %copy-start.1 = (bf16[16,1024,128]{2,1,0:T(8,128)(2,1)S(1)}, bf16[16,1024,128]{2,1,0:T(8,128)(2,1)}, u32[]{:S(2)}) copy-start(bf16[16,1024,128]{2,1,0:T(8,128)(2,1)} %get-tuple-element.10.filt_ref) | copy-start | bytes 12582916
  123.0 0.8 copy-start.12
  125.8 19.7 %all-to-all-start.4 = ((bf16[8,256,128]{1,2,0:T(8,128)(2,1)}), bf16[8,256,128]{1,2,0:T(8,128)(2,1)}, u32[]{:S(2)}, u32[]{:S(2)}) async-start(bf16[8,256,128]{1,2,0:T(8,128)(2,1)} %copy.15), calls=%async_computation.4 | async-start | bytes 1048576 | tf_op jit(solution)/shard_map/all_to_all | solution.py:220
  130.9 18.9 %collective-permute-start.1 = (bf16[4,2048]{1,0:T(4,128)(2,1)S(1)}, bf16[4,2048]{1,0:T(4,128)(2,1)S(1)}, u32[]{:S(2)}, u32[]{:S(2)}) collective-permute-start(bf16[4,2048]{1,0:T(4,128)(2,1)S(1)} %pad_maximum_fusion.1), channel_id=1, source_target_pairs={{4,0},{8,4},{12,8},{16,12},{20,16},{24,20},{28,24},{5,1},{9,5},{13... | collective-permute-start | bytes 49160 | tf_op jit(solution)/shard_map/ppermute | solution.py:18
  133.9 0.8 copy-start.10
  134.7 15.2 %collective-permute-start.2 = (bf16[2,2048]{1,0:T(2,128)(2,1)S(1)}, bf16[2,2048]{1,0:T(2,128)(2,1)S(1)}, u32[]{:S(2)}, u32[]{:S(2)}) collective-permute-start(bf16[2,2048]{1,0:T(2,128)(2,1)S(1)} %slice.28), channel_id=1, source_target_pairs={{4,0},{8,4},{12,8},{16,12},{20,16},{24,20},{28,24},{5,1},{9,5},{13... | collective-permute-start | bytes 24584 | tf_op jit(solution)/shard_map/ppermute | solution.py:18
  146.6 5.0 %collective-permute-start.3 = (bf16[2,2048]{1,0:T(2,128)(2,1)S(1)}, bf16[2,2048]{1,0:T(2,128)(2,1)S(1)}, u32[]{:S(2)}, u32[]{:S(2)}) collective-permute-start(bf16[2,2048]{1,0:T(2,128)(2,1)S(1)} %slice_bitcast_fusion), channel_id=1, source_target_pairs={{4,0},{8,4},{12,8},{16,12},{20,16},{24,20},{28,24},{5,1},{9,5},{13... | collective-permute-start | bytes 24584 | tf_op jit(solution)/shard_map/ppermute | solution.py:18
  151.6 1.0 copy-start.5
  152.7 1.0 copy-start.7
  153.7 1.0 copy-start.11
Sparse Core Ops, SparseCore 0:
  72.0 46.7 all-gather.1

commit v2 on v0

v2 whole, which is shorter than its diff:
```python
import jax
import jax.numpy as jnp
from jax import lax
from jax.experimental import pallas as pl
from jax.experimental.pallas import tpu as pltpu
from jax.sharding import PartitionSpec as P

GROUP = 16
F32 = jnp.float32
BF16 = jnp.bfloat16
MESH = pl.DeviceIdType.MESH


def causal(x, before, taps):
    row = lax.broadcasted_iota(jnp.int32, x.shape, 0)
    one = jnp.where(row == 0, before[1:2], pltpu.roll(x, 1, 0))
    two = jnp.where(row == 0, before[0:1], jnp.where(row == 1, before[1:2], pltpu.roll(x, 2, 0)))
    return x * taps[0:1] + one * taps[1:2] + two * taps[2:3]


def anticausal(g, after, taps):
    count = g.shape[0]
    row = lax.broadcasted_iota(jnp.int32, g.shape, 0)
    one = jnp.where(row == count - 1, after[0:1], pltpu.roll(g, count - 1, 0))
    two = jnp.where(
        row == count - 1,
        after[1:2],
        jnp.where(row == count - 2, after[0:1], pltpu.roll(g, count - 2, 0)),
    )
    return g * taps[0:1] + one * taps[1:2] + two * taps[2:3]


def rounded(x):
    return x.astype(BF16).astype(F32)


def step_kernel(
    q_ref, k_ref, v_ref, taps_ref, h_ref, hr_ref, w_hbm, go_ref,
    out_ref, gq_ref, gk_ref, gv_ref,
    w_ref, got_ref, filt_ref, send_refs, recv_refs, part_send, part_recv, gall_ref, acc_ref,
    gqf_ref, gp_ref, hsend_ref, hrecv_ref, tail_ref, head_ref,
    w_sem, seq_send, seq_recv, chan_send, chan_recv, halo_send, halo_recv,
):
    seq = lax.axis_size("seq")
    chan = lax.axis_size("chan")
    here = lax.axis_index("seq")
    mine = lax.axis_index("chan")
    count, width = q_ref.shape
    _, groups, gw, _ = recv_refs.shape[1:]
    per = groups * gw
    length = h_ref.shape[1]
    columns = go_ref.shape[1]
    tile = max(per, min(256, width))
    tiles = width // tile
    dests = tile // per
    rows = min(512, width)
    wide = min(512, columns)

    def seq_peer(off):
        return lax.rem(here + off, seq)

    def chan_peer(off):
        return lax.rem(mine + off, chan)

    def w_copy(off):
        at = pl.ds(pl.multiple_of(chan_peer(off) * width, width), width)
        return pltpu.make_async_copy(w_hbm.at[at], w_ref.at[at], w_sem.at[off])

    order = [off % chan for off in range(1, chan + 1)]
    for off in order:
        w_copy(off).start()

    barrier = pltpu.get_barrier_semaphore()

    def greet_seq(off, carry):
        pl.semaphore_signal(
            barrier, inc=1, device_id={"seq": seq_peer(off)}, device_id_type=MESH
        )
        return carry

    def greet_chan(off, carry):
        pl.semaphore_signal(
            barrier, inc=1, device_id={"chan": chan_peer(off)}, device_id_type=MESH
        )
        return carry

    lax.fori_loop(1, seq, greet_seq, 0)
    lax.fori_loop(1, chan, greet_chan, 0)

    for m, ref in enumerate((q_ref, k_ref, v_ref)):
        hsend_ref[0, 2 * m : 2 * m + 2, :] = ref[count - 16 :, :].astype(F32)[14:]
        hsend_ref[1, 2 * m : 2 * m + 2, :] = ref[:16, :].astype(F32)[:2]
    pl.semaphore_wait(barrier, seq + chan - 2)

    def halo(slot, by, src, dst):
        return pltpu.make_async_remote_copy(
            src_ref=src, dst_ref=dst, send_sem=halo_send.at[slot], recv_sem=halo_recv.at[slot],
            device_id={"seq": seq_peer(by)}, device_id_type=MESH,
        )

    halo_down = halo(0, 1, hsend_ref.at[0, 0:6], hrecv_ref.at[0, 0:6])
    halo_up = halo(1, seq - 1, hsend_ref.at[1, 0:6], hrecv_ref.at[1, 0:6])
    halo_down.start()
    halo_up.start()

    def turn(i, carry):
        at = pl.ds(pl.multiple_of(i * wide, wide), wide)
        got_ref[at, :] = go_ref[:, at].astype(F32).T.astype(BF16)
        return carry

    lax.fori_loop(0, columns // wide, turn, 0)

    def exchange(slot, off):
        return pltpu.make_async_remote_copy(
            src_ref=send_refs.at[slot, seq_peer(off)],
            dst_ref=recv_refs.at[slot, here],
            send_sem=seq_send.at[slot, off],
            recv_sem=seq_recv.at[slot, off],
            device_id={"seq": seq_peer(off)},
            device_id_type=MESH,
        )

    def exchange_start(slot):
        def go(off, carry):
            exchange(slot, off).start()
            return carry

        lax.fori_loop(1, seq, go, 0)
        recv_refs[slot, pl.ds(here, 1)] = send_refs[slot, pl.ds(here, 1)]

    def exchange_wait(slot):
        def go(off, carry):
            exchange(slot, off).wait()
            return carry

        lax.fori_loop(1, seq, go, 0)

    def to_send(slot, i, turned):
        send_refs[slot, pl.ds(i * dests, dests)] = turned.reshape(
            dests, groups, gw, count
        ).astype(BF16)

    def from_recv(slot, i):
        return recv_refs[slot, pl.ds(i * dests, dests)].astype(F32).reshape(tile, count)

    def cols(i):
        return pl.ds(pl.multiple_of(i * tile, tile), tile)

    def filtered(ref, m, at):
        ahead = jnp.where(here > 0, hrecv_ref[0, 2 * m : 2 * m + 2, at], 0.0)
        return causal(ref[:, at].astype(F32), ahead, taps_ref[3 * m : 3 * m + 3, at])

    halo_down.wait()
    halo_up.wait()

    def products(i, carry):
        at = cols(i)
        to_send(0, i, (filtered(k_ref, 1, at) * filtered(v_ref, 2, at)).T)
        return carry

    lax.fori_loop(0, tiles, products, 0)
    exchange_start(0)

    def part(off):
        return pltpu.make_async_remote_copy(
            src_ref=part_send.at[off - 1],
            dst_ref=part_recv.at[mine],
            send_sem=chan_send.at[0, off],
            recv_sem=chan_recv.at[0, off],
            device_id={"chan": chan_peer(off)},
            device_id_type=MESH,
        )

    for off in order:
        w_copy(off).wait()

        def some(i, carry, off=off):
            start = pl.multiple_of(chan_peer(off) * width + i * rows, rows)
            got = jnp.dot(w_ref[pl.ds(start, rows), :], got_ref[...], preferred_element_type=F32)
            at = pl.ds(pl.multiple_of(i * rows, rows), rows)
            if off:
                part_send[off - 1, at, :] = got.astype(BF16)
            else:
                part_recv[mine, at, :] = got.astype(BF16)
            return carry

        lax.fori_loop(0, width // rows, some, 0)
        if off:
            part(off).start()

    def build(forward):
        def one(g, carry):
            pad = jnp.zeros((count, count), F32)
            row = (h_ref if forward else hr_ref)[pl.ds(g, 1), :]
            lines = jnp.broadcast_to(row, (count, length))
            pair = [pad, lines] if forward else [lines, pad]
            lined = pltpu.roll(
                jnp.concatenate(pair, axis=1), 0 if forward else 1, 1, stride=1, stride_axis=0
            ).astype(BF16)
            for k in range(length // count):
                at = (k + 1) * count if forward else length - k * count
                filt_ref[g, k * count : (k + 1) * count, :] = lined[:, at : at + count]
            return carry

        lax.fori_loop(0, groups, one, 0)

    def mix(forward, slot):
        total_rows = seq * gw

        def one(g, carry):
            x = recv_refs[slot, :, g]
            kind = F32 if gw % 16 else BF16
            x = x.astype(kind).reshape(total_rows, count)
            pieces = [x.astype(BF16)]
            for k in range(1, seq):
                pad = jnp.zeros((k * gw, count), kind)
                if forward:
                    moved = jnp.concatenate([pad, x[: total_rows - k * gw]], axis=0)
                else:
                    moved = jnp.concatenate([x[k * gw :], pad], axis=0)
                pieces.append(moved.astype(BF16))
            total = jnp.dot(
                jnp.concatenate(pieces, axis=1), filt_ref[g], preferred_element_type=F32
            )
            send_refs[slot + 1, :, g] = total.reshape(seq, gw, count).astype(BF16)
            return carry

        lax.fori_loop(0, groups, one, 0)

    build(True)
    exchange_wait(0)
    mix(True, 0)
    exchange_start(1)
    build(False)

    for off in range(1, chan):
        part(off).wait()

    def summed(at):
        return jnp.sum(part_recv[:, at, :].astype(F32), axis=0)

    def grad_mixed(i, carry):
        at = cols(i)
        to_send(2, i, summed(at) * filtered(q_ref, 0, at).T)
        return carry

    lax.fori_loop(0, tiles, grad_mixed, 0)
    exchange_start(2)

    def share(off):
        return pltpu.make_async_remote_copy(
            src_ref=gall_ref.at[mine],
            dst_ref=gall_ref.at[mine],
            send_sem=chan_send.at[1, off],
            recv_sem=chan_recv.at[1, off],
            device_id={"chan": chan_peer(off)},
            device_id_type=MESH,
        )

    exchange_wait(1)

    def gate(i, carry):
        at = cols(i)
        gall_ref[mine, :, at] = (filtered(q_ref, 0, at) * from_recv(1, i).T).astype(BF16)
        return carry

    lax.fori_loop(0, tiles, gate, 0)
    for off in range(1, chan):
        share(off).start()

    def grad_query(i, carry):
        at = cols(i)
        gqf_ref[:, at] = rounded((summed(at) * from_recv(1, i)).T)
        return carry

    lax.fori_loop(0, tiles, grad_query, 0)

    def project(off, first, last):
        owner = chan_peer(chan - off)

        def some(i, carry):
            at = pl.ds(pl.multiple_of(i * wide, wide), wide)
            start = pl.multiple_of(owner * width, width)
            got = jnp.dot(
                gall_ref[owner], w_ref[pl.ds(start, width), at], preferred_element_type=F32
            )
            if not first:
                got = got + acc_ref[:, at]
            if last:
                out_ref[:, at] = got.astype(BF16)
            else:
                acc_ref[:, at] = got
            return carry

        lax.fori_loop(0, columns // wide, some, 0)

    project(0, True, chan == 1)
    exchange_wait(2)
    mix(False, 2)
    exchange_start(3)
    for off in range(1, chan):
        share(off).wait()
        project(off, False, off == chan - 1)

    exchange_wait(3)

    def grad_products(i, carry):
        at = cols(i)
        gp_ref[:, at] = from_recv(3, i).T
        return carry

    lax.fori_loop(0, tiles, grad_products, 0)
    tail_ref[0:2, :] = gqf_ref[0:2, :]
    tail_ref[2:4, :] = gp_ref[0:2, :]
    tail = halo(2, seq - 1, tail_ref, head_ref)
    tail.start()
    tail.wait()

    def last(i, carry):
        at = cols(i)

        def behind(ref, m):
            x = ref[count - 16 :, at].astype(F32)
            taps = taps_ref[3 * m : 3 * m + 3, at]
            new = hrecv_ref[1, 2 * m : 2 * m + 2, at]
            first = new[0:1] * taps[0:1] + x[15:16] * taps[1:2] + x[14:15] * taps[2:3]
            second = new[1:2] * taps[0:1] + new[0:1] * taps[1:2] + x[15:16] * taps[2:3]
            return jnp.concatenate([first, second], axis=0)

        def masked(rows_after):
            return jnp.where(here < seq - 1, rows_after, 0.0)

        gp = gp_ref[:, at]
        gp_next = head_ref[2:4, at]
        gq_ref[:, at] = anticausal(
            gqf_ref[:, at], masked(head_ref[0:2, at]), taps_ref[0:3, at]
        ).astype(BF16)
        gk_ref[:, at] = anticausal(
            rounded(gp * filtered(v_ref, 2, at)),
            masked(rounded(gp_next * behind(v_ref, 2))),
            taps_ref[3:6, at],
        ).astype(BF16)
        gv_ref[:, at] = anticausal(
            rounded(gp * filtered(k_ref, 1, at)),
            masked(rounded(gp_next * behind(k_ref, 1))),
            taps_ref[6:9, at],
        ).astype(BF16)
        return carry

    lax.fori_loop(0, tiles, last, 0)


def local(query_proj, key_proj, value_proj, short_filter, long_filter, out_weight, grad_out):
    count, width = query_proj.shape
    seq = lax.axis_size("seq")
    chan = lax.axis_size("chan")
    per = width // seq
    gw = min(per, GROUP)
    groups = per // gw
    length = long_filter.shape[1]
    depth, columns = out_weight.shape

    taps = jnp.repeat(short_filter.transpose(0, 2, 1).reshape(9, -1), GROUP, axis=1)
    first = lax.axis_index("seq") * per // GROUP
    chosen = lax.dynamic_slice_in_dim(long_filter, first, groups, 0).astype(F32)

    vmem = pl.BlockSpec(memory_space=pltpu.VMEM)
    flat = jax.ShapeDtypeStruct((count, width), BF16)
    return pl.pallas_call(
        step_kernel,
        in_specs=[vmem] * 6 + [pl.BlockSpec(memory_space=pl.ANY), vmem],
        out_specs=[vmem] * 4,
        out_shape=[jax.ShapeDtypeStruct((count, columns), BF16), flat, flat, flat],
        scratch_shapes=[
            pltpu.VMEM((depth, columns), BF16),
            pltpu.VMEM((columns, count), BF16),
            pltpu.VMEM((groups, length, count), BF16),
            pltpu.VMEM((4, seq, groups, gw, count), BF16),
            pltpu.VMEM((4, seq, groups, gw, count), BF16),
            pltpu.VMEM((chan - 1, width, count), BF16),
            pltpu.VMEM((chan, width, count), BF16),
            pltpu.VMEM((chan, count, width), BF16),
            pltpu.VMEM((count, columns), F32),
            pltpu.VMEM((count, width), F32),
            pltpu.VMEM((count, width), F32),
            pltpu.VMEM((2, 8, width), F32),
            pltpu.VMEM((2, 8, width), F32),
            pltpu.VMEM((4, width), F32),
            pltpu.VMEM((4, width), F32),
            pltpu.SemaphoreType.DMA((chan,)),
            pltpu.SemaphoreType.DMA((4, seq)),
            pltpu.SemaphoreType.DMA((4, seq)),
            pltpu.SemaphoreType.DMA((2, chan)),
            pltpu.SemaphoreType.DMA((2, chan)),
            pltpu.SemaphoreType.DMA((3,)),
            pltpu.SemaphoreType.DMA((3,)),
        ],
        compiler_params=pltpu.CompilerParams(
            collective_id=0, has_side_effects=True, vmem_limit_bytes=62 * 1024 * 1024
        ),
        name="step",
    )(query_proj, key_proj, value_proj, taps, chosen, chosen[:, ::-1], out_weight, grad_out)


def solution(mesh):
    return jax.shard_map(
        local,
        mesh=mesh,
        in_specs=(
            P("seq", "chan"),
            P("seq", "chan"),
            P("seq", "chan"),
            P(None, "chan", None),
            P("chan", None),
            P(None, "chan"),
            P("seq", "chan"),
        ),
        out_specs=(P("seq", "chan"), P("seq", "chan"), P("seq", "chan"), P("seq", "chan")),
        check_vma=False,
    )
```

time: 2210 us -> 91 us (0.04)
  local copies, waits for them, and re-layouts: 1970 us -> 12.2 us
  waiting for transfers between devices: 86.8 us -> 0 us
  Pallas kernels: 0 us -> 76.8 us
  matrix products: 54.8 us -> 0 us
  blocking collectives: 35.3 us -> 0 us
    gather x16 -> x0, local copies, waits for them, and re-layouts: 1940 us -> none  [add_lag(): kernel = window[:, offsets]]
    pallas_call x0 -> x1, Pallas kernels: none -> 76.8 us  [local(): pl.pallas_call(step_kernel, in_specs=[vmem] * 6 + [pl.BlockSpec(memory_sp...]
    dot_general x10 -> x0, matrix products: 54.8 us -> none  [the longest x8 21.3 us: add_lag(): jnp.einsum('gab,gjnb->gjna', kernel, source, preferred_element_type=jnp.f...]
    reduce_scatter x1 -> x0, waiting for transfers between devices: 37.6 us -> none  [backward_partials(): lax.psum_scatter(lax.dot_general(out_weight, grad_out, (((1,), (1,)), (()...]
    all_to_all x2 -> x0, blocking collectives: 35.3 us -> none  [to_tokens(): lax.all_to_all(values, 'seq', split_axis=0, concat_axis=1, tiled=True)]
    all_to_all x2 -> x0, waiting for transfers between devices: 28 us -> none  [to_channels(): lax.all_to_all(values, 'seq', split_axis=1, concat_axis=0, tiled=True)]
  transfers between devices with their start and end apart: 6 -> 0, of which waited for: 6 -> 0; matrix products, arithmetic and copies ran while one was open for 1% -> 0% of each run, Pallas kernels for 0% -> 0%
where the time goes in v2:
time: 91 us; the launch traced here: 90.6 us
  Pallas kernels  76.8 us (84%)
  local copies, waits for them, and re-layouts  12.2 us (13%)
    pallas_call x1, Pallas kernels, local(): pl.pallas_call(step_kernel, in_specs=[vmem] * 6 + [pl.BlockSpec(memory_sp...  76.8 us
    unnamed x6, local copies, waits for them, and re-layouts  7.53 us
    rev x1, local copies, waits for them, and re-layouts, local(): chosen[:, ::-1]  2.78 us

profile of v2, /device:TPU:1, one launch (start us, length us, event | category | flops | bytes accessed | tf_op | source)
XLA Modules:
  0.0 90.6 jit_solution(3337174691201967255)
XLA Ops:
  0.7 0.7 reshape.14
  1.4 0.8 dynamic-slice_convert_fusion.h_ref
  2.2 0.0 copy-start
  2.2 2.8 %rev.3.hr_ref = f32[16,1024]{1,0:T(8,128)} reverse(f32[16,1024]{1,0:T(8,128)S(1)} %dynamic-slice_convert_fusion.h_ref), dimensions={1} | reverse | bytes 131072 | tf_op jit(solution)/shard_map/rev | solution.py:402
  5.0 0.2 broadcast_in_dim.3
  5.2 1.0 %reshape.15.taps_ref = f32[9,2048]{1,0:T(8,128)} reshape(f32[9,128,16]{2,1,0:T(8,128)S(1)} %broadcast_in_dim.3) | data formatting | bytes 147456 | tf_op jit(solution)/shard_map/reshape | solution.py:363
  6.2 0.0 copy-done
  6.2 76.8 %step.1 = (bf16[128,2048]{1,0:T(8,128)(2,1)}, bf16[128,2048]{1,0:T(8,128)(2,1)}, bf16[128,2048]{1,0:T(8,128)(2,1)}, bf16[128,2048]{1,0:T(8,128)(2,1)}) custom-call(bf16[128,2048]{1,0:T(8,128)(2,1)} %q_ref.1, bf16[128,2048]{1,0:T(8,128)(2,1)} %k_ref.1, bf16[128,2048]{1,0:T(8,128)(2,1)} %v_ref.1, f32[9,2048]{1,0:T(8,128)} %reshape.15.taps_ref, ...), custom_call_target="tpu_custom_call" | custom-call | tf_op jit(solution)/shard_map/step/pallas_call | solution.py:369
  83.0 1.9 %copy.15 = bf16[128,2048]{1,0:T(8,128)(2,1)} copy(bf16[128,2048]{1,0:T(8,128)(2,1)} %get-tuple-element.8) | data formatting | bytes 1048576
  84.9 1.9 %copy.16 = bf16[128,2048]{1,0:T(8,128)(2,1)} copy(bf16[128,2048]{1,0:T(8,128)(2,1)} %get-tuple-element.9) | data formatting | bytes 1048576
  86.8 1.9 %copy.17 = bf16[128,2048]{1,0:T(8,128)(2,1)} copy(bf16[128,2048]{1,0:T(8,128)(2,1)} %get-tuple-element.10) | data formatting | bytes 1048576
  88.7 1.9 %copy.18 = bf16[128,2048]{1,0:T(8,128)(2,1)} copy(bf16[128,2048]{1,0:T(8,128)(2,1)} %get-tuple-element.11) | data formatting | bytes 1048576
Async XLA Ops:
  2.2 4.0 %copy-start = (f32[16,1024]{1,0:T(8,128)}, f32[16,1024]{1,0:T(8,128)S(1)}, u32[]{:S(2)}) copy-start(f32[16,1024]{1,0:T(8,128)S(1)} %dynamic-slice_convert_fusion.h_ref) | copy-start | bytes 196612

commit v3 on v2

--- a/solution.py
+++ b/solution.py
@@ -35,10 +35,10 @@
 
 
 def step_kernel(
-    q_ref, k_ref, v_ref, taps_ref, h_ref, hr_ref, w_hbm, go_ref,
-    out_ref, gq_ref, gk_ref, gv_ref,
-    w_ref, got_ref, filt_ref, send_refs, recv_refs, part_send, part_recv, gall_ref, acc_ref,
-    gqf_ref, gp_ref, hsend_ref, hrecv_ref, tail_ref, head_ref,
+    q_ref, k_ref, v_ref, taps_ref, h_ref, w_hbm, go_ref,
+    out_ref, gqf_ref, gp_ref, before_ref, after_ref,
+    w_ref, got_ref, hr_ref, filt_ref, send_refs, recv_refs, part_send, part_recv, gall_ref,
+    acc_ref, hsend_ref, hrecv_ref, tail_ref, head_ref,
     w_sem, seq_send, seq_recv, chan_send, chan_recv, halo_send, halo_recv,
 ):
     seq = lax.axis_size("seq")
@@ -171,10 +171,10 @@
             device_id_type=MESH,
         )
 
-    for off in order:
+    def back_project(off):
         w_copy(off).wait()
 
-        def some(i, carry, off=off):
+        def some(i, carry):
             start = pl.multiple_of(chan_peer(off) * width + i * rows, rows)
             got = jnp.dot(w_ref[pl.ds(start, rows), :], got_ref[...], preferred_element_type=F32)
             at = pl.ds(pl.multiple_of(i * rows, rows), rows)
@@ -187,6 +187,20 @@
         lax.fori_loop(0, width // rows, some, 0)
         if off:
             part(off).start()
+
+    for off in range(1, chan):
+        back_project(off)
+
+    flip = (
+        lax.broadcasted_iota(jnp.int32, (count, count), 0)
+        + lax.broadcasted_iota(jnp.int32, (count, count), 1)
+        == count - 1
+    )
+    flip = jnp.where(flip, 1.0, 0.0).astype(BF16)
+    for k in range(length // count):
+        hr_ref[:, length - (k + 1) * count : length - k * count] = jnp.dot(
+            h_ref[:, k * count : (k + 1) * count].astype(BF16), flip, preferred_element_type=F32
+        )
 
     def build(forward):
         def one(g, carry):
@@ -231,6 +245,7 @@
     exchange_wait(0)
     mix(True, 0)
     exchange_start(1)
+    back_project(0)
     build(False)
 
     for off in range(1, chan):
@@ -270,7 +285,7 @@
 
     def grad_query(i, carry):
         at = cols(i)
-        gqf_ref[:, at] = rounded((summed(at) * from_recv(1, i)).T)
+        gqf_ref[:, at] = (summed(at) * from_recv(1, i)).T.astype(BF16)
         return carry
 
     lax.fori_loop(0, tiles, grad_query, 0)
@@ -306,48 +321,49 @@
 
     def grad_products(i, carry):
         at = cols(i)
-        gp_ref[:, at] = from_recv(3, i).T
+        gp_ref[:, at] = from_recv(3, i).T.astype(BF16)
         return carry
 
     lax.fori_loop(0, tiles, grad_products, 0)
-    tail_ref[0:2, :] = gqf_ref[0:2, :]
-    tail_ref[2:4, :] = gp_ref[0:2, :]
+    tail_ref[0:2, :] = gqf_ref[:16, :].astype(F32)[:2]
+    tail_ref[2:4, :] = gp_ref[:16, :].astype(F32)[:2]
     tail = halo(2, seq - 1, tail_ref, head_ref)
     tail.start()
+    before_ref[0:6, :] = jnp.where(here > 0, hrecv_ref[0, 0:6, :], 0.0)
+    after_ref[4:8, :] = hrecv_ref[1, 2:6, :]
     tail.wait()
-
-    def last(i, carry):
-        at = cols(i)
-
-        def behind(ref, m):
-            x = ref[count - 16 :, at].astype(F32)
-            taps = taps_ref[3 * m : 3 * m + 3, at]
-            new = hrecv_ref[1, 2 * m : 2 * m + 2, at]
-            first = new[0:1] * taps[0:1] + x[15:16] * taps[1:2] + x[14:15] * taps[2:3]
-            second = new[1:2] * taps[0:1] + new[0:1] * taps[1:2] + x[15:16] * taps[2:3]
-            return jnp.concatenate([first, second], axis=0)
-
-        def masked(rows_after):
-            return jnp.where(here < seq - 1, rows_after, 0.0)
-
-        gp = gp_ref[:, at]
-        gp_next = head_ref[2:4, at]
-        gq_ref[:, at] = anticausal(
-            gqf_ref[:, at], masked(head_ref[0:2, at]), taps_ref[0:3, at]
-        ).astype(BF16)
-        gk_ref[:, at] = anticausal(
-            rounded(gp * filtered(v_ref, 2, at)),
-            masked(rounded(gp_next * behind(v_ref, 2))),
-            taps_ref[3:6, at],
-        ).astype(BF16)
-        gv_ref[:, at] = anticausal(
-            rounded(gp * filtered(k_ref, 1, at)),
-            masked(rounded(gp_next * behind(k_ref, 1))),
-            taps_ref[6:9, at],
-        ).astype(BF16)
-        return carry
-
-    lax.fori_loop(0, tiles, last, 0)
+    after_ref[0:4, :] = jnp.where(here < seq - 1, head_ref[...], 0.0)
+
+
+def last_kernel(
+    k_ref, v_ref, taps_ref, mixer_ref, gqf_ref, gp_ref, before_ref, after_ref,
+    out_ref, gq_ref, gk_ref, gv_ref,
+):
+    count = k_ref.shape[0]
+    gp = gp_ref[...].astype(F32)
+    gqf_next = after_ref[0:2]
+    gp_next = after_ref[2:4]
+
+    def both(ref, m):
+        x = ref[...].astype(F32)
+        taps = taps_ref[3 * m : 3 * m + 3]
+        new = after_ref[2 + 2 * m : 4 + 2 * m]
+        near, far = x[count - 1 : count], x[count - 2 : count - 1]
+        first = new[0:1] * taps[0:1] + near * taps[1:2] + far * taps[2:3]
+        second = new[1:2] * taps[0:1] + new[0:1] * taps[1:2] + near * taps[2:3]
+        inside = causal(x, before_ref[2 * m : 2 * m + 2], taps)
+        return inside, jnp.concatenate([first, second], axis=0)
+
+    kf, kf_next = both(k_ref, 1)
+    vf, vf_next = both(v_ref, 2)
+    out_ref[...] = mixer_ref[...]
+    gq_ref[...] = anticausal(gqf_ref[...].astype(F32), gqf_next, taps_ref[0:3]).astype(BF16)
+    gk_ref[...] = anticausal(
+        rounded(gp * vf), rounded(gp_next * vf_next), taps_ref[3:6]
+    ).astype(BF16)
+    gv_ref[...] = anticausal(
+        rounded(gp * kf), rounded(gp_next * kf_next), taps_ref[6:9]
+    ).astype(BF16)
 
 
 def local(query_proj, key_proj, value_proj, short_filter, long_filter, out_weight, grad_out):
@@ -366,14 +382,16 @@
 
     vmem = pl.BlockSpec(memory_space=pltpu.VMEM)
     flat = jax.ShapeDtypeStruct((count, width), BF16)
-    return pl.pallas_call(
+    rims = jax.ShapeDtypeStruct((8, width), F32)
+    mixer_out, grad_qf, grad_prod, before, after = pl.pallas_call(
         step_kernel,
-        in_specs=[vmem] * 6 + [pl.BlockSpec(memory_space=pl.ANY), vmem],
-        out_specs=[vmem] * 4,
-        out_shape=[jax.ShapeDtypeStruct((count, columns), BF16), flat, flat, flat],
+        in_specs=[vmem] * 5 + [pl.BlockSpec(memory_space=pl.ANY), vmem],
+        out_specs=[vmem] * 5,
+        out_shape=[jax.ShapeDtypeStruct((count, columns), BF16), flat, flat, rims, rims],
         scratch_shapes=[
             pltpu.VMEM((depth, columns), BF16),
             pltpu.VMEM((columns, count), BF16),
+            pltpu.VMEM((groups, length), F32),
             pltpu.VMEM((groups, length, count), BF16),
             pltpu.VMEM((4, seq, groups, gw, count), BF16),
             pltpu.VMEM((4, seq, groups, gw, count), BF16),
@@ -381,8 +399,6 @@
             pltpu.VMEM((chan, width, count), BF16),
             pltpu.VMEM((chan, count, width), BF16),
             pltpu.VMEM((count, columns), F32),
-            pltpu.VMEM((count, width), F32),
-            pltpu.VMEM((count, width), F32),
             pltpu.VMEM((2, 8, width), F32),
             pltpu.VMEM((2, 8, width), F32),
             pltpu.VMEM((4, width), F32),
@@ -399,7 +415,22 @@
             collective_id=0, has_side_effects=True, vmem_limit_bytes=62 * 1024 * 1024
         ),
         name="step",
-    )(query_proj, key_proj, value_proj, taps, chosen, chosen[:, ::-1], out_weight, grad_out)
+    )(query_proj, key_proj, value_proj, taps, chosen, out_weight, grad_out)
+
+    tile = min(512, width)
+
+    def tall(rows):
+        return pl.BlockSpec((rows, tile), lambda i: (0, i))
+
+    return pl.pallas_call(
+        last_kernel,
+        grid=(width // tile,),
+        in_specs=[tall(count), tall(count), tall(9)] + [tall(count)] * 3 + [tall(8)] * 2,
+        out_specs=[tall(count)] * 4,
+        out_shape=[flat] * 4,
+        compiler_params=pltpu.CompilerParams(vmem_limit_bytes=32 * 1024 * 1024),
+        name="last",
+    )(key_proj, value_proj, taps, mixer_out, grad_qf, grad_prod, before, after)
 
 
 def solution(mesh):

time: 91 us -> 87.2 us (0.958)
  local copies, waits for them, and re-layouts: 12.2 us -> 6.8 us
    rev x1 -> x0, local copies, waits for them, and re-layouts: 2.78 us -> none  [local(): chosen[:, ::-1]]
    unnamed x6 -> x16, local copies, waits for them, and re-layouts: 7.53 us -> 4.81 us
    pallas_call x1 -> x2, Pallas kernels: 76.8 us -> 77.3 us  [the longest x1 74.1 us: local(): pl.pallas_call(step_kernel, in_specs=[vmem] * 5 + [pl.BlockSpec(memory_sp...]
where the time goes in v3:
time: 87.2 us; the launch traced here: 86.3 us
  Pallas kernels  77.3 us (89%)
  local copies, waits for them, and re-layouts  6.8 us (8%)
  other arithmetic  1.44 us (2%)
    pallas_call x1, Pallas kernels, local(): pl.pallas_call(step_kernel, in_specs=[vmem] * 5 + [pl.BlockSpec(memory_sp...  74.1 us
    unnamed x16, local copies, waits for them, and re-layouts  4.81 us
    pallas_call x1, Pallas kernels, local(): pl.pallas_call(last_kernel, grid=(width // tile,), in_specs=[tall(count),...  3.23 us

profile of v3, /device:TPU:1, one launch (start us, length us, event | category | flops | bytes accessed | tf_op | source)
XLA Modules:
  0.0 86.3 jit_solution(2486734919494455121)
XLA Ops:
  0.6 0.0 copy-start.1
  0.6 0.0 copy-start
  0.7 0.8 reshape.14
  1.5 1.4 %dynamic-slice_convert_fusion.h_ref = f32[16,1024]{1,0:T(8,128)} fusion(bf16[128,1024]{1,0:T(8,128)(2,1)} %param.11, s32[]{:T(128)S(6)} %select_n.9), kind=kLoop, calls=%fused_computation | loop fusion | flops 16384 | bytes 98308 | tf_op jit(solution)/shard_map/convert_element_type | solution.py:381
  2.9 0.2 broadcast_in_dim.3
  3.1 1.0 %reshape.15.taps_ref = f32[9,2048]{1,0:T(8,128)} reshape(f32[9,128,16]{2,1,0:T(8,128)S(1)} %broadcast_in_dim.3) | data formatting | bytes 147456 | tf_op jit(solution)/shard_map/reshape | solution.py:379
  4.1 0.0 copy-start.2
  4.1 74.1 %step.1 = (bf16[128,2048]{1,0:T(8,128)(2,1)}, bf16[128,2048]{1,0:T(8,128)(2,1)}, bf16[128,2048]{1,0:T(8,128)(2,1)}, f32[8,2048]{1,0:T(8,128)}, f32[8,2048]{1,0:T(8,128)}) custom-call(bf16[128,2048]{1,0:T(8,128)(2,1)} %q_ref.1, bf16[128,2048]{1,0:T(8,128)(2,1)} %k_ref.3, bf16[128,2048]{1,0:T(8,128)(2,1)} %v_ref.3, f32[9,2048]{1,0:T(8,128)} %reshape.15.taps_ref, ...), custom_call_target="tpu_custom_call" | custom-call | tf_op jit(solution)/shard_map/step/pallas_call | solution.py:386
  78.2 0.0 copy-done.1
  78.2 0.0 copy-done
  78.2 0.0 copy-done.2
  78.2 0.0 copy-start.3
  78.2 1.0 %copy-done.3 = bf16[128,2048]{1,0:T(8,128)(2,1)S(1)} copy-done((bf16[128,2048]{1,0:T(8,128)(2,1)S(1)}, bf16[128,2048]{1,0:T(8,128)(2,1)}, u32[]{:S(2)}) %copy-start.3) | copy-done | bytes 524312
  79.3 0.0 copy-start.4
  79.3 1.0 %copy-done.4 = bf16[128,2048]{1,0:T(8,128)(2,1)S(1)} copy-done((bf16[128,2048]{1,0:T(8,128)(2,1)S(1)}, bf16[128,2048]{1,0:T(8,128)(2,1)}, u32[]{:S(2)}) %copy-start.4) | copy-done | bytes 524312
  80.3 0.0 copy-start.5
  80.3 1.0 %copy-done.5 = bf16[128,2048]{1,0:T(8,128)(2,1)S(1)} copy-done((bf16[128,2048]{1,0:T(8,128)(2,1)S(1)}, bf16[128,2048]{1,0:T(8,128)(2,1)}, u32[]{:S(2)}) %copy-start.5) | copy-done | bytes 524312
  81.4 0.0 copy-start.6
  81.4 0.8 copy-done.6
  82.2 0.0 copy-start.7
  82.2 0.8 copy-done.7
  83.0 3.2 %last.1 = (bf16[128,2048]{1,0:T(8,128)(2,1)}, bf16[128,2048]{1,0:T(8,128)(2,1)}, bf16[128,2048]{1,0:T(8,128)(2,1)}, bf16[128,2048]{1,0:T(8,128)(2,1)}) custom-call(bf16[128,2048]{1,0:T(8,128)(2,1)S(1)} %copy-done, bf16[128,2048]{1,0:T(8,128)(2,1)S(1)} %copy-done.1, f32[9,2048]{1,0:T(8,128)S(1)} %copy-done.2, bf16[128,2048]{1,0:T(8,128)(2,1)S(1)} %copy-done.3, ...), custom_call_target="tpu_custom_call" | custom-call | tf_op jit(solution)/shard_map/last/pallas_call | solution.py:425
Async XLA Ops:
  0.6 77.6 %copy-start.1 = (bf16[128,2048]{1,0:T(8,128)(2,1)S(1)}, bf16[128,2048]{1,0:T(8,128)(2,1)}, u32[]{:S(2)}) copy-start(bf16[128,2048]{1,0:T(8,128)(2,1)} %v_ref.3) | copy-start | bytes 1572868
  0.6 77.6 %copy-start = (bf16[128,2048]{1,0:T(8,128)(2,1)S(1)}, bf16[128,2048]{1,0:T(8,128)(2,1)}, u32[]{:S(2)}) copy-start(bf16[128,2048]{1,0:T(8,128)(2,1)} %k_ref.3) | copy-start | bytes 1572868
  4.1 74.1 %copy-start.2 = (f32[9,2048]{1,0:T(8,128)S(1)}, f32[9,2048]{1,0:T(8,128)}, u32[]{:S(2)}) copy-start(f32[9,2048]{1,0:T(8,128)} %reshape.15.taps_ref) | copy-start | bytes 221188
  78.2 1.0 %copy-start.3 = (bf16[128,2048]{1,0:T(8,128)(2,1)S(1)}, bf16[128,2048]{1,0:T(8,128)(2,1)}, u32[]{:S(2)}) copy-start(bf16[128,2048]{1,0:T(8,128)(2,1)} %get-tuple-element.9.mixer_ref) | copy-start | bytes 1572868
  79.3 1.0 %copy-start.4 = (bf16[128,2048]{1,0:T(8,128)(2,1)S(1)}, bf16[128,2048]{1,0:T(8,128)(2,1)}, u32[]{:S(2)}) copy-start(bf16[128,2048]{1,0:T(8,128)(2,1)} %get-tuple-element.10.gqf_ref) | copy-start | bytes 1572868
  80.3 1.0 %copy-start.5 = (bf16[128,2048]{1,0:T(8,128)(2,1)S(1)}, bf16[128,2048]{1,0:T(8,128)(2,1)}, u32[]{:S(2)}) copy-start(bf16[128,2048]{1,0:T(8,128)(2,1)} %get-tuple-element.11.gp_ref) | copy-start | bytes 1572868
  81.4 0.8 copy-start.6
  82.2 0.8 copy-start.7

commit v4 on v3

--- a/solution.py
+++ b/solution.py
@@ -153,13 +153,25 @@
     halo_down.wait()
     halo_up.wait()
 
-    def products(i, carry):
-        at = cols(i)
-        to_send(0, i, (filtered(k_ref, 1, at) * filtered(v_ref, 2, at)).T)
-        return carry
-
-    lax.fori_loop(0, tiles, products, 0)
-    exchange_start(0)
+    def spread(slot, make):
+        def one(i, carry):
+            to_send(slot, i, make(cols(i)))
+            return carry
+
+        def off_to(off, carry):
+            one(seq_peer(off), 0)
+            exchange(slot, off).start()
+            return carry
+
+        if dests == 1:
+            lax.fori_loop(1, seq, off_to, 0)
+            one(here, 0)
+            recv_refs[slot, pl.ds(here, 1)] = send_refs[slot, pl.ds(here, 1)]
+        else:
+            lax.fori_loop(0, tiles, one, 0)
+            exchange_start(slot)
+
+    spread(0, lambda at: (filtered(k_ref, 1, at) * filtered(v_ref, 2, at)).T)
 
     def part(off):
         return pltpu.make_async_remote_copy(
@@ -254,13 +266,7 @@
     def summed(at):
         return jnp.sum(part_recv[:, at, :].astype(F32), axis=0)
 
-    def grad_mixed(i, carry):
-        at = cols(i)
-        to_send(2, i, summed(at) * filtered(q_ref, 0, at).T)
-        return carry
-
-    lax.fori_loop(0, tiles, grad_mixed, 0)
-    exchange_start(2)
+    spread(2, lambda at: summed(at) * filtered(q_ref, 0, at).T)
 
     def share(off):
         return pltpu.make_async_remote_copy(
@@ -428,7 +434,7 @@
         in_specs=[tall(count), tall(count), tall(9)] + [tall(count)] * 3 + [tall(8)] * 2,
         out_specs=[tall(count)] * 4,
         out_shape=[flat] * 4,
-        compiler_params=pltpu.CompilerParams(vmem_limit_bytes=32 * 1024 * 1024),
+        compiler_params=pltpu.CompilerParams(vmem_limit_bytes=62 * 1024 * 1024),
         name="last",
     )(key_proj, value_proj, taps, mixer_out, grad_qf, grad_prod, before, after)
 

time: 87.2 us -> 83.6 us (0.959)
  local copies, waits for them, and re-layouts: 6.8 us -> 1.9 us
  Pallas kernels: 77.3 us -> 78.8 us
    unnamed x16 -> x0, local copies, waits for them, and re-layouts: 4.81 us -> none
    pallas_call x1, Pallas kernels: 3.23 us -> 4.91 us  [local(): pl.pallas_call(last_kernel, grid=(width // tile,), in_specs=[tall(count),...]
where the time goes in v4:
time: 83.6 us; the launch traced here: 82.8 us
  Pallas kernels  78.8 us (94%)
  local copies, waits for them, and re-layouts  1.9 us (2%)
  other arithmetic  1.44 us (2%)
    pallas_call x1, Pallas kernels, local(): pl.pallas_call(step_kernel, in_specs=[vmem] * 5 + [pl.BlockSpec(memory_sp...  73.9 us
    pallas_call x1, Pallas kernels, local(): pl.pallas_call(last_kernel, grid=(width // tile,), in_specs=[tall(count),...  4.91 us

profile of v4, /device:TPU:1, one launch (start us, length us, event | category | flops | bytes accessed | tf_op | source)
XLA Modules:
  0.0 82.8 jit_solution(17892960507867581204)
XLA Ops:
  0.7 0.7 reshape.14
  1.4 1.4 %dynamic-slice_convert_fusion.h_ref = f32[16,1024]{1,0:T(8,128)} fusion(bf16[128,1024]{1,0:T(8,128)(2,1)} %param.11, s32[]{:T(128)S(6)} %select_n.9), kind=kLoop, calls=%fused_computation | loop fusion | flops 16384 | bytes 98308 | tf_op jit(solution)/shard_map/convert_element_type | solution.py:387
  2.8 0.2 broadcast_in_dim.3
  3.0 1.0 %reshape.15.taps_ref = f32[9,2048]{1,0:T(8,128)} reshape(f32[9,128,16]{2,1,0:T(8,128)S(1)} %broadcast_in_dim.3) | data formatting | bytes 147456 | tf_op jit(solution)/shard_map/reshape | solution.py:385
  4.0 73.9 %step.1 = (bf16[128,2048]{1,0:T(8,128)(2,1)}, bf16[128,2048]{1,0:T(8,128)(2,1)}, bf16[128,2048]{1,0:T(8,128)(2,1)}, f32[8,2048]{1,0:T(8,128)}, f32[8,2048]{1,0:T(8,128)}) custom-call(bf16[128,2048]{1,0:T(8,128)(2,1)} %q_ref.1, bf16[128,2048]{1,0:T(8,128)(2,1)} %k_ref.3, bf16[128,2048]{1,0:T(8,128)(2,1)} %v_ref.3, f32[9,2048]{1,0:T(8,128)} %reshape.15.taps_ref, ...), custom_call_target="tpu_custom_call" | custom-call | tf_op jit(solution)/shard_map/step/pallas_call | solution.py:392
  77.9 4.9 %last.1 = (bf16[128,2048]{1,0:T(8,128)(2,1)}, bf16[128,2048]{1,0:T(8,128)(2,1)}, bf16[128,2048]{1,0:T(8,128)(2,1)}, bf16[128,2048]{1,0:T(8,128)(2,1)}) custom-call(bf16[128,2048]{1,0:T(8,128)(2,1)} %k_ref.3, bf16[128,2048]{1,0:T(8,128)(2,1)} %v_ref.3, f32[9,2048]{1,0:T(8,128)} %reshape.15.taps_ref, bf16[128,2048]{1,0:T(8,128)(2,1)} %get-tuple-element.9.mixer_ref, ...), custom_call_target="tpu_custom_call" | custom-call | tf_op jit(solution)/shard_map/last/pallas_call | solution.py:431

commit v5 on v4

--- a/solution.py
+++ b/solution.py
@@ -150,59 +150,6 @@
         ahead = jnp.where(here > 0, hrecv_ref[0, 2 * m : 2 * m + 2, at], 0.0)
         return causal(ref[:, at].astype(F32), ahead, taps_ref[3 * m : 3 * m + 3, at])
 
-    halo_down.wait()
-    halo_up.wait()
-
-    def spread(slot, make):
-        def one(i, carry):
-            to_send(slot, i, make(cols(i)))
-            return carry
-
-        def off_to(off, carry):
-            one(seq_peer(off), 0)
-            exchange(slot, off).start()
-            return carry
-
-        if dests == 1:
-            lax.fori_loop(1, seq, off_to, 0)
-            one(here, 0)
-            recv_refs[slot, pl.ds(here, 1)] = send_refs[slot, pl.ds(here, 1)]
-        else:
-            lax.fori_loop(0, tiles, one, 0)
-            exchange_start(slot)
-
-    spread(0, lambda at: (filtered(k_ref, 1, at) * filtered(v_ref, 2, at)).T)
-
-    def part(off):
-        return pltpu.make_async_remote_copy(
-            src_ref=part_send.at[off - 1],
-            dst_ref=part_recv.at[mine],
-            send_sem=chan_send.at[0, off],
-            recv_sem=chan_recv.at[0, off],
-            device_id={"chan": chan_peer(off)},
-            device_id_type=MESH,
-        )
-
-    def back_project(off):
-        w_copy(off).wait()
-
-        def some(i, carry):
-            start = pl.multiple_of(chan_peer(off) * width + i * rows, rows)
-            got = jnp.dot(w_ref[pl.ds(start, rows), :], got_ref[...], preferred_element_type=F32)
-            at = pl.ds(pl.multiple_of(i * rows, rows), rows)
-            if off:
-                part_send[off - 1, at, :] = got.astype(BF16)
-            else:
-                part_recv[mine, at, :] = got.astype(BF16)
-            return carry
-
-        lax.fori_loop(0, width // rows, some, 0)
-        if off:
-            part(off).start()
-
-    for off in range(1, chan):
-        back_project(off)
-
     flip = (
         lax.broadcasted_iota(jnp.int32, (count, count), 0)
         + lax.broadcasted_iota(jnp.int32, (count, count), 1)
@@ -229,6 +176,60 @@
             return carry
 
         lax.fori_loop(0, groups, one, 0)
+
+    build(True)
+    halo_down.wait()
+    halo_up.wait()
+
+    def spread(slot, make):
+        def one(i, carry):
+            to_send(slot, i, make(cols(i)))
+            return carry
+
+        def off_to(off, carry):
+            one(seq_peer(off), 0)
+            exchange(slot, off).start()
+            return carry
+
+        if dests == 1:
+            lax.fori_loop(1, seq, off_to, 0)
+            one(here, 0)
+            recv_refs[slot, pl.ds(here, 1)] = send_refs[slot, pl.ds(here, 1)]
+        else:
+            lax.fori_loop(0, tiles, one, 0)
+            exchange_start(slot)
+
+    spread(0, lambda at: (filtered(k_ref, 1, at) * filtered(v_ref, 2, at)).T)
+
+    def part(off):
+        return pltpu.make_async_remote_copy(
+            src_ref=part_send.at[off - 1],
+            dst_ref=part_recv.at[mine],
+            send_sem=chan_send.at[0, off],
+            recv_sem=chan_recv.at[0, off],
+            device_id={"chan": chan_peer(off)},
+            device_id_type=MESH,
+        )
+
+    def back_project(off):
+        w_copy(off).wait()
+
+        def some(i, carry):
+            start = pl.multiple_of(chan_peer(off) * width + i * rows, rows)
+            got = jnp.dot(w_ref[pl.ds(start, rows), :], got_ref[...], preferred_element_type=F32)
+            at = pl.ds(pl.multiple_of(i * rows, rows), rows)
+            if off:
+                part_send[off - 1, at, :] = got.astype(BF16)
+            else:
+                part_recv[mine, at, :] = got.astype(BF16)
+            return carry
+
+        lax.fori_loop(0, width // rows, some, 0)
+        if off:
+            part(off).start()
+
+    for off in range(1, chan):
+        back_project(off)
 
     def mix(forward, slot):
         total_rows = seq * gw
@@ -253,7 +254,6 @@
 
         lax.fori_loop(0, groups, one, 0)
 
-    build(True)
     exchange_wait(0)
     mix(True, 0)
     exchange_start(1)

time: 83.6 us -> 84 us (level)
  Pallas kernels: 78.8 us -> 79.7 us
    pallas_call x1, Pallas kernels: 73.9 us -> 74.8 us  [local(): pl.pallas_call(step_kernel, in_specs=[vmem] * 5 + [pl.BlockSpec(memory_sp...]
where the time goes in v5:
time: 84 us; the launch traced here: 83.7 us
  Pallas kernels  79.7 us (95%)
  local copies, waits for them, and re-layouts  1.9 us (2%)
  other arithmetic  1.44 us (2%)
    pallas_call x1, Pallas kernels, local(): pl.pallas_call(step_kernel, in_specs=[vmem] * 5 + [pl.BlockSpec(memory_sp...  74.8 us
    pallas_call x1, Pallas kernels, local(): pl.pallas_call(last_kernel, grid=(width // tile,), in_specs=[tall(count),...  4.91 us

profile of v5, /device:TPU:1, one launch (start us, length us, event | category | flops | bytes accessed | tf_op | source)
XLA Modules:
  0.0 83.7 jit_solution(843371217981139582)
XLA Ops:
  0.7 0.7 reshape.14
  1.4 1.4 %dynamic-slice_convert_fusion.h_ref = f32[16,1024]{1,0:T(8,128)} fusion(bf16[128,1024]{1,0:T(8,128)(2,1)} %param.11, s32[]{:T(128)S(6)} %select_n.9), kind=kLoop, calls=%fused_computation | loop fusion | flops 16384 | bytes 98308 | tf_op jit(solution)/shard_map/convert_element_type | solution.py:387
  2.8 0.2 broadcast_in_dim.3
  3.0 1.0 %reshape.15.taps_ref = f32[9,2048]{1,0:T(8,128)} reshape(f32[9,128,16]{2,1,0:T(8,128)S(1)} %broadcast_in_dim.3) | data formatting | bytes 147456 | tf_op jit(solution)/shard_map/reshape | solution.py:385
  4.0 74.8 %step.1 = (bf16[128,2048]{1,0:T(8,128)(2,1)}, bf16[128,2048]{1,0:T(8,128)(2,1)}, bf16[128,2048]{1,0:T(8,128)(2,1)}, f32[8,2048]{1,0:T(8,128)}, f32[8,2048]{1,0:T(8,128)}) custom-call(bf16[128,2048]{1,0:T(8,128)(2,1)} %q_ref.1, bf16[128,2048]{1,0:T(8,128)(2,1)} %k_ref.3, bf16[128,2048]{1,0:T(8,128)(2,1)} %v_ref.3, f32[9,2048]{1,0:T(8,128)} %reshape.15.taps_ref, ...), custom_call_target="tpu_custom_call" | custom-call | tf_op jit(solution)/shard_map/step/pallas_call | solution.py:392
  78.8 4.9 %last.1 = (bf16[128,2048]{1,0:T(8,128)(2,1)}, bf16[128,2048]{1,0:T(8,128)(2,1)}, bf16[128,2048]{1,0:T(8,128)(2,1)}, bf16[128,2048]{1,0:T(8,128)(2,1)}) custom-call(bf16[128,2048]{1,0:T(8,128)(2,1)} %k_ref.3, bf16[128,2048]{1,0:T(8,128)(2,1)} %v_ref.3, f32[9,2048]{1,0:T(8,128)} %reshape.15.taps_ref, bf16[128,2048]{1,0:T(8,128)(2,1)} %get-tuple-element.9.mixer_ref, ...), custom_call_target="tpu_custom_call" | custom-call | tf_op jit(solution)/shard_map/last/pallas_call | solution.py:431
